TPU v7x, 128 devices: a whole 4x4x4 slice. The times are simulated.
128 devices in a mesh: dp: 8 (over z, core), mp: 16 (over y, x).
Axes of the slice: x: 4, y: 4, z: 4, core: 2. Of those that a mesh axis runs over, the one named last changes fastest.
Arguments:
- stream: bfloat16 [65536, 2048], P(('dp', 'mp')), may hold values from -5.5 to 5.5
- norm_weight: float32 [2048], replicated, may hold values from 0.5 to 1.5
- query_key_weight: bfloat16 [2048, 512], P(('dp', 'mp')), may hold values from -0.25 to 0.25
- value_weight: bfloat16 [2048, 2048], P(('dp', 'mp')), may hold values from -0.125 to 0.125
- output_weight: bfloat16 [2048, 2048], P(('dp', 'mp')), may hold values from -0.5 to 0.5
- convolution_weights: float32 [3, 2048], replicated, may hold values from -2.5 to 2.5
- adapter_down_maps: bfloat16 [64, 16, 2048], P('mp'), may hold values from -0.125 to 0.125
- adapter_up_maps: bfloat16 [64, 16, 2048], P('mp'), may hold values from -1.5 to 1.5
- prompt_lengths: int32 [128, 8], P(('dp', 'mp')), may hold values from 1 to 256, 512 in all within a row
- block_adapter_index: int32 [2048], P(('dp', 'mp')), may hold values from 0 to 63, as said below
Outputs:
- hidden: bfloat16 [65536, 2048], P(('dp', 'mp'))
Inputs may be any that keep to these rules, and one draw needn't show every extreme that they name: `prompt_lengths`: each row holds the lengths of one device's 8 prompts; a row sums to 512 and its largest entry is exactly 256. `block_adapter_index`: adapters k * 4 to (k + 1) * 4 - 1 sit on index k of mp. The 16 blocks of one device name adapters of any one index of mp at most 2 times; in every draw, on each index of dp, one index of mp is named exactly 2 times by every device.
All inputs are finite; a program needn't handle non-finite values.
Results may differ from a plain program's by a relative error of at most 0.0088.
Values may be sent and summed in bfloat16 or wider, within the bound.
A program may use at most 128 MiB of HBM per device.

v0:
```python
import math

import jax
import jax.numpy as jnp
from jax import lax
from jax.sharding import PartitionSpec as P

HEADS = 16
QK = 16


adapter_scale = 2.0
norm_eps = 1e-05


def prompt_index(lengths, total_token_count):
    bounds = jnp.cumsum(lengths)
    position = jnp.arange(total_token_count, dtype=jnp.int32)
    return jnp.sum((position[:, None] >= bounds[None, :]).astype(jnp.int32), axis=1)


def short_conv(value_matrix, tap_table, segment):
    result = tap_table[0][None, :] * value_matrix
    for offset in range(1, tap_table.shape[0]):
        earlier = jnp.concatenate(
            [jnp.zeros((offset, value_matrix.shape[1]), jnp.float32), value_matrix[:-offset]],
            axis=0,
        )
        same_prompt = jnp.concatenate(
            [jnp.zeros((offset,), jnp.bool_), segment[offset:] == segment[:-offset]], axis=0
        )
        result = result + tap_table[offset][None, :] * jnp.where(same_prompt[:, None], earlier, 0.0)
    return result


def taylor_heads(query_key, mixed, segment, head_count, feature):
    total_token_count, hidden_width = mixed.shape
    head_width = hidden_width // head_count
    queries = (
        query_key[:, : head_count * feature]
        .reshape(total_token_count, head_count, feature)
        .transpose(1, 0, 2)
    )
    key_rows = (
        query_key[:, head_count * feature :]
        .reshape(total_token_count, head_count, feature)
        .transpose(1, 0, 2)
    )
    value_rows = mixed.reshape(total_token_count, head_count, head_width).transpose(1, 0, 2)
    position = jnp.arange(total_token_count, dtype=jnp.int32)
    allowed = (position[None, :] <= position[:, None]) & (segment[None, :] == segment[:, None])
    score_scale = 1.0 / math.sqrt(feature)

    def one_head(operands):
        query_one, key_one, value_one = operands
        scores = jnp.dot(query_one, key_one.T, preferred_element_type=jnp.float32) * score_scale
        weight = jnp.where(allowed, 1.0 + scores + 0.5 * scores * scores, 0.0)
        row_total = jnp.sum(weight, axis=1, keepdims=True)
        numerator = jnp.dot(
            weight.astype(jnp.bfloat16), value_one, preferred_element_type=jnp.float32
        )
        return numerator / row_total

    outputs = lax.map(one_head, (queries, key_rows, value_rows))
    return outputs.transpose(1, 0, 2).reshape(total_token_count, hidden_width).astype(jnp.bfloat16)


def local(
    stream,
    norm_weight,
    query_key_weight,
    value_weight,
    output_weight,
    convolution_weights,
    adapter_down_maps,
    adapter_up_maps,
    prompt_lengths,
    block_adapter_index,
):
    total_token_count, hidden_width = stream.shape
    stream_f = stream.astype(jnp.float32)
    mean_sq = jnp.mean(stream_f * stream_f, axis=1, keepdims=True)
    normed = (stream_f * lax.rsqrt(mean_sq + norm_eps) * norm_weight[None, :]).astype(jnp.bfloat16)
    inputs = normed
    qk_sum = jnp.dot(
        inputs,
        lax.all_gather(query_key_weight, ("dp", "mp"), axis=0, tiled=True),
        preferred_element_type=jnp.float32,
    )
    plain_value_rows = jnp.dot(
        inputs,
        lax.all_gather(value_weight, ("dp", "mp"), axis=0, tiled=True),
        preferred_element_type=jnp.float32,
    )
    query_key = qk_sum.astype(jnp.bfloat16)
    holders = lax.axis_size("mp")
    local_token_count = adapter_down_maps.shape[0]
    adapter_width = adapter_down_maps.shape[1]
    block_count = block_adapter_index.shape[0]
    block_rows = total_token_count // block_count
    capacity = 2 * block_count // holders
    holder_of = block_adapter_index // local_token_count
    within = (block_adapter_index % local_token_count).astype(jnp.float32)
    onehot = (holder_of[:, None] == jnp.arange(holders, dtype=jnp.int32)[None, :]).astype(jnp.int32)
    slot_index = jnp.sum((jnp.cumsum(onehot, axis=0) - 1) * onehot, axis=1)
    target = holder_of * capacity + slot_index
    select = (jnp.arange(holders * capacity, dtype=jnp.int32)[:, None] == target[None, :]).astype(
        jnp.bfloat16
    )
    outgoing = jnp.dot(
        select,
        normed.reshape(block_count, block_rows * hidden_width),
        preferred_element_type=jnp.float32,
    )
    outgoing = outgoing.astype(jnp.bfloat16).reshape(holders, capacity * block_rows, hidden_width)
    slot_local = jnp.dot(select.astype(jnp.float32), within, preferred_element_type=jnp.float32)
    slot_local = (
        jnp.repeat(slot_local, block_rows)
        .astype(jnp.bfloat16)
        .reshape(holders, capacity * block_rows)
    )
    flattened_down = adapter_down_maps.reshape(local_token_count * adapter_width, hidden_width)
    flattened_up = adapter_up_maps.reshape(local_token_count * adapter_width, hidden_width)
    column_owner = (
        jnp.arange(local_token_count * adapter_width, dtype=jnp.int32) // adapter_width
    ).astype(jnp.float32)
    rows_here = lax.all_to_all(outgoing, "mp", split_axis=0, concat_axis=0, tiled=True)
    local_ids = lax.all_to_all(slot_local, "mp", split_axis=0, concat_axis=0, tiled=True)
    low_all = jnp.einsum(
        "skd,cd->skc", rows_here, flattened_down, preferred_element_type=jnp.float32
    )
    keep = local_ids.astype(jnp.float32)[:, :, None] == column_owner[None, None, :]
    reduced_rows = jnp.where(keep, low_all, 0.0).astype(jnp.bfloat16)
    value_update = adapter_scale * jnp.einsum(
        "skc,cd->skd", reduced_rows, flattened_up, preferred_element_type=jnp.float32
    )
    returned = lax.all_to_all(
        value_update.astype(jnp.bfloat16), "mp", split_axis=0, concat_axis=0, tiled=True
    )
    adapter_delta = jnp.dot(
        select.T,
        returned.reshape(holders * capacity, block_rows * hidden_width),
        preferred_element_type=jnp.float32,
    )
    adapter_delta = adapter_delta.reshape(total_token_count, hidden_width)
    value_matrix = plain_value_rows + adapter_delta
    segment = prompt_index(prompt_lengths[0], total_token_count)
    conv = short_conv(value_matrix, convolution_weights, segment)
    mixed = (conv * jax.nn.silu(value_matrix)).astype(jnp.bfloat16)
    attended = taylor_heads(query_key, mixed, segment, HEADS, QK)
    inputs = attended
    projected = jnp.dot(
        inputs,
        lax.all_gather(output_weight, ("dp", "mp"), axis=0, tiled=True),
        preferred_element_type=jnp.float32,
    )
    return (stream_f + projected).astype(jnp.bfloat16)


def solution(mesh):
    return jax.shard_map(
        local,
        mesh=mesh,
        in_specs=(
            P(("dp", "mp"), None),
            P(),
            P(("dp", "mp"), None),
            P(("dp", "mp"), None),
            P(("dp", "mp"), None),
            P(),
            P("mp", None, None),
            P("mp", None, None),
            P(("dp", "mp"), None),
            P(("dp", "mp")),
        ),
        out_specs=P(("dp", "mp"), None),
        check_vma=False,
    )
```

profile of v0, /device:TPU:1, one launch (start us, length us, event | category | flops | bytes accessed | tf_op | source)
XLA Modules:
  0.0 303.8 jit_solution(3091795847900209915)
XLA Ops:
  6.5 0.7 all-gather.4.cloned.1.call-update
  7.3 0.7 all-gather.6.cloned.1.call-update
  9.6 0.8 fusion.19
  10.6 0.7 convert_element_type.107
  11.3 7.6 %all-to-all-start = ((bf16[16,1,64]{2,1,0:T(2,128)(2,1)}), bf16[16,1,64]{2,1,0:T(2,128)(2,1)S(1)}, u32[]{:S(2)}, u32[]{:S(2)}) async-start(bf16[16,1,64]{2,1,0:T(2,128)(2,1)} %convert_element_type.107), calls=%async_computation | async-start | bytes 16384 | tf_op jit(solution)/shard_map/all_to_all | solution.py:128
  18.9 2.1 fusion.13
  21.0 3.5 %fusion.15 = bf16[512,2048]{1,0:T(8,128)(2,1)} fusion(bf16[512,2048]{1,0:T(8,128)(2,1)} %param.12, f32[2048]{0:T(1024)} %param.13, f32[512]{0:T(512)S(1)} %add_rsqrt_fusion), kind=kLoop, calls=%fused_computation.23 | loop fusion | flops 4194304 | bytes 4204544 | tf_op jit(solution)/shard_map/convert_element_type | solution.py:83
  24.4 2.2 reshape.118
  26.6 3.2 %convolution_convert_fusion = bf16[32,65536]{1,0:T(8,128)(2,1)} fusion(bf16[16,65536]{1,0:T(8,128)(2,1)S(1)} %reshape.118, s32[16]{0:T(128)S(1)} %multiply_add_fusion), kind=kOutput, calls=%fused_computation.16 | convolution fusion | flops 69206528 | bytes 6291520 | tf_op jit(solution)/shard_map/dot_general | solution.py:110
  29.8 5.6 %reshape.119 = bf16[16,64,2048]{2,1,0:T(8,128)(2,1)} reshape(bf16[32,65536]{1,0:T(8,128)(2,1)} %convolution_convert_fusion) | data formatting | bytes 8388608 | tf_op jit(solution)/shard_map/reshape | solution.py:115
  35.5 6.8 %all-to-all-start.1 = ((bf16[16,64,2048]{2,1,0:T(8,128)(2,1)}), bf16[16,64,2048]{2,1,0:T(8,128)(2,1)}, u32[]{:S(2)}, u32[]{:S(2)}) async-start(bf16[16,64,2048]{2,1,0:T(8,128)(2,1)} %reshape.119), calls=%async_computation.1 | async-start | bytes 8388608 | tf_op jit(solution)/shard_map/all_to_all | solution.py:127
  42.3 0.7 all-gather.8.cloned.1.call-update
  43.1 61.8 %all-to-all-done.1 = bf16[16,64,2048]{2,1,0:T(8,128)(2,1)} async-done(((bf16[16,64,2048]{2,1,0:T(8,128)(2,1)}), bf16[16,64,2048]{2,1,0:T(8,128)(2,1)}, u32[]{:S(2)}, u32[]{:S(2)}) %all-to-all-start.1) | async-done | bytes 4194336 | tf_op jit(solution)/shard_map/all_to_all | solution.py:127
  104.8 8.5 %multiply_convert_fusion = bf16[16,64,2048]{2,1,0:T(8,128)(2,1)} fusion(bf16[64,2048,1]{1,0,2:T(8,128)(2,1)S(1)} %bitcast.74, bf16[16,64,2048]{2,1,0:T(8,128)(2,1)} %all-to-all-done.1, bf16[64,2048,1]{1,0,2:T(8,128)(2,1)S(1)} %bitcast.79, f32[64]{0:T(128)S(1)} %fusion.29, f32[16,64]{1,0:T(8,128)S(1)} %bitcast.83), kind=kOutput, calls=%fused_computation.17 | convolution fusion | flops 541261824 | bytes 8917248 | tf_op jit(solution)/shard_map/skc,cd->skd/dot_general | solution.py:134
  113.4 4.9 %all-to-all-start.2 = ((bf16[16,64,2048]{2,1,0:T(8,128)(2,1)}), bf16[16,64,2048]{2,1,0:T(8,128)(2,1)}, u32[]{:S(2)}, u32[]{:S(2)}) async-start(bf16[16,64,2048]{2,1,0:T(8,128)(2,1)} %multiply_convert_fusion), calls=%async_computation.2 | async-start | bytes 8388608 | tf_op jit(solution)/shard_map/all_to_all | solution.py:137
  118.9 2.9 convolution_convert_fusion.1
  121.9 53.5 %all-to-all-done.2 = bf16[16,64,2048]{2,1,0:T(8,128)(2,1)} async-done(((bf16[16,64,2048]{2,1,0:T(8,128)(2,1)}), bf16[16,64,2048]{2,1,0:T(8,128)(2,1)}, u32[]{:S(2)}, u32[]{:S(2)}) %all-to-all-start.2) | async-done | bytes 4194336 | tf_op jit(solution)/shard_map/all_to_all | solution.py:137
  175.3 5.7 %reshape.122 = bf16[32,65536]{1,0:T(8,128)(2,1)} reshape(bf16[16,64,2048]{2,1,0:T(8,128)(2,1)} %all-to-all-done.2) | data formatting | bytes 8388608 | tf_op jit(solution)/shard_map/reshape | solution.py:142
  181.0 5.0 %fusion.24 = f32[16,65536]{1,0:T(8,128)} fusion(bf16[32,65536]{1,0:T(8,128)(2,1)} %reshape.122, s32[16]{0:T(128)S(1)} %multiply_add_fusion), kind=kOutput, calls=%fused_computation.39 | convolution fusion | flops 67109376 | bytes 8388672 | tf_op jit(solution)/shard_map/dot_general | solution.py:140
  186.0 4.0 %reshape.123 = f32[512,2048]{1,0:T(8,128)} reshape(f32[16,65536]{1,0:T(8,128)} %fusion.24) | data formatting | bytes 8388608 | tf_op jit(solution)/shard_map/reshape | solution.py:145
  189.9 27.0 %all-gather.6.cloned.1.call-done = bf16[2048,2048]{1,0:T(8,128)(2,1)} async-done(((bf16[16,2048]{1,0:T(8,128)(2,1)}), bf16[2048,2048]{1,0:T(8,128)(2,1)}) %all-gather.6.cloned.1.call-update) | async-done | bytes 8388624 | tf_op jit(solution)/shard_map/all_gather | solution.py:92
  216.9 8.7 %convolution_add_fusion = f32[512,2048]{1,0:T(8,128)S(1)} fusion(f32[512,2048]{1,0:T(8,128)} %reshape.123, bf16[512,2048]{1,0:T(8,128)(2,1)S(1)} %copy-done.3, bf16[2048,2048]{1,0:T(8,128)(2,1)} %all-gather.6.cloned.1.call-done), kind=kOutput, calls=%fused_computation.26 | convolution fusion | flops 4296015872 | bytes 18874368 | tf_op jit(solution)/shard_map/dot_general | solution.py:90
  225.6 4.3 %bitcast_bitcast_fusion = bf16[16,512,128]{2,1,0:T(8,128)(2,1)} fusion(f32[512,2048]{1,0:T(8,128)S(1)} %convolution_add_fusion, f32[510,2048]{1,0:T(8,128)S(1)} %bitcast.75, pred[512]{0:T(512)(128)(4,1)S(1)} %concatenate.14, f32[2048]{0:T(1024)S(1)} %bitcast.81, f32[511,2048]{1,0:T(8,128)S(1)} %bitcast.76, pred[512]{0:T(512)(128)(4,1)S(1)} %pad_add_fusion, ...), kind=kLoop, calls=%fused_computation.27 | loop fusion | flops 13631488 | bytes 14681088 | tf_op jit(solution)/shard_map/transpose | solution.py:49
  230.0 40.6 %while.13 = (s32[]{:T(128)}, bf16[16,512,128]{1,2,0:T(8,128)(2,1)}, bf16[16,512,16]{1,2,0:T(8,128)(2,1)S(1)}, bf16[16,512,16]{1,2,0:T(8,128)(2,1)S(1)}, bf16[16,...) while((s32[]{:T(128)}, bf16[16,512,128]{1,2,0:T(8,128)(2,1)}, ...), condition=%wide.region_7.8_spmd.clone, body=%wide.region_5.7_spmd.clone.sunk | while | flops 78511616 | bytes 1878093 | solution.py:64
  230.4 1.4 fusion.61
  232.0 0.7 constant_dynamic-update-slice_fusion.2
  233.1 1.3 fusion.61
  235.7 1.3 fusion.61
  238.2 1.3 fusion.61
  240.7 1.3 fusion.61
  243.2 1.3 fusion.61
  244.6 0.7 constant_dynamic-update-slice_fusion.2
  245.8 1.3 fusion.61
  248.3 1.3 fusion.61
  249.7 0.7 constant_dynamic-update-slice_fusion.2
  250.8 1.3 fusion.61
  252.2 0.7 constant_dynamic-update-slice_fusion.2
  253.4 1.3 fusion.61
  255.9 1.3 fusion.61
  257.3 0.7 constant_dynamic-update-slice_fusion.2
  258.4 1.3 fusion.61
  261.0 1.3 fusion.61
  263.5 1.3 fusion.61
  266.0 1.3 fusion.61
  268.5 1.3 fusion.61
  269.9 0.7 constant_dynamic-update-slice_fusion.2
  270.6 16.7 %all-gather.8.cloned.1.call-done = bf16[2048,2048]{1,0:T(8,128)(2,1)} async-done(((bf16[16,2048]{1,0:T(8,128)(2,1)}), bf16[2048,2048]{1,0:T(8,128)(2,1)}) %all-gather.8.cloned.1.call-update) | async-done | bytes 8388624 | tf_op jit(solution)/shard_map/all_gather | solution.py:154
  287.3 9.9 %fusion.16 = bf16[512,2048]{1,0:T(8,128)(2,1)} fusion(bf16[512,2048]{1,0:T(8,128)(2,1)S(1)} %copy-done.2, bf16[512,2048]{0,1:T(8,128)(2,1)} %bitcast.85, bf16[2048,2048]{1,0:T(8,128)(2,1)} %all-gather.8.cloned.1.call-done), kind=kOutput, calls=%fused_computation.24 | convolution fusion | flops 4298113024 | bytes 14680064 | tf_op jit(solution)/shard_map/dot_general | solution.py:152
  (80 shorter events, 18.6 us)
Async XLA Ops:
  6.5 98.3 %copy-start = (bf16[4,16,2048]{2,1,0:T(8,128)(2,1)S(1)}, bf16[4,16,2048]{2,1,0:T(8,128)(2,1)}, u32[]{:S(2)}) copy-start(bf16[4,16,2048]{2,1,0:T(8,128)(2,1)} %param.19) | copy-start | bytes 786436
  6.5 112.4 %all-gather.4.cloned.1.call-start = ((), (), s32[]{:S(2)}) async-start(), calls=%async_computation.3 | async-start | bytes 2113536 | tf_op jit(solution)/shard_map/all_gather | solution.py:87
  7.3 209.6 %all-gather.6.cloned.1.call-start = ((), (), s32[]{:S(2)}) async-start(), calls=%async_computation.4 | async-start | bytes 8454144 | tf_op jit(solution)/shard_map/all_gather | solution.py:92
  11.3 24.2 %all-to-all-start = ((bf16[16,1,64]{2,1,0:T(2,128)(2,1)}), bf16[16,1,64]{2,1,0:T(2,128)(2,1)S(1)}, u32[]{:S(2)}, u32[]{:S(2)}) async-start(bf16[16,1,64]{2,1,0:T(2,128)(2,1)} %convert_element_type.107), calls=%async_computation | async-start | bytes 16384 | tf_op jit(solution)/shard_map/all_to_all | solution.py:128
  35.4 69.4 %copy-start.4 = (bf16[4,16,2048]{2,1,0:T(8,128)(2,1)S(1)}, bf16[4,16,2048]{2,1,0:T(8,128)(2,1)}, u32[]{:S(2)}) copy-start(bf16[4,16,2048]{2,1,0:T(8,128)(2,1)} %param.18) | copy-start | bytes 786436
  35.5 69.4 %all-to-all-start.1 = ((bf16[16,64,2048]{2,1,0:T(8,128)(2,1)}), bf16[16,64,2048]{2,1,0:T(8,128)(2,1)}, u32[]{:S(2)}, u32[]{:S(2)}) async-start(bf16[16,64,2048]{2,1,0:T(8,128)(2,1)} %reshape.119), calls=%async_computation.1 | async-start | bytes 8388608 | tf_op jit(solution)/shard_map/all_to_all | solution.py:127
  42.3 245.0 %all-gather.8.cloned.1.call-start = ((), (), s32[]{:S(2)}) async-start(), calls=%async_computation.5 | async-start | bytes 8454144 | tf_op jit(solution)/shard_map/all_gather | solution.py:154
  113.4 4.9 %copy-start.6 = (s32[1,8]{1,0:T(1,128)S(1)}, s32[1,8]{1,0:T(1,128)}, u32[]{:S(2)}) copy-start(s32[1,8]{1,0:T(1,128)} %param.20) | copy-start | bytes 100
  113.4 5.5 %copy-start.5 = (f32[3,2048]{1,0:T(4,128)S(1)}, f32[3,2048]{1,0:T(4,128)}, u32[]{:S(2)}) copy-start(f32[3,2048]{1,0:T(4,128)} %param.17) | copy-start | bytes 73732
  113.4 5.5 %copy-start.3 = (bf16[512,2048]{1,0:T(8,128)(2,1)S(1)}, bf16[512,2048]{1,0:T(8,128)(2,1)}, u32[]{:S(2)}) copy-start(bf16[512,2048]{1,0:T(8,128)(2,1)} %fusion.15) | copy-start | bytes 6291460
  113.4 62.0 %all-to-all-start.2 = ((bf16[16,64,2048]{2,1,0:T(8,128)(2,1)}), bf16[16,64,2048]{2,1,0:T(8,128)(2,1)}, u32[]{:S(2)}, u32[]{:S(2)}) async-start(bf16[16,64,2048]{2,1,0:T(8,128)(2,1)} %multiply_convert_fusion), calls=%async_computation.2 | async-start | bytes 8388608 | tf_op jit(solution)/shard_map/all_to_all | solution.py:137
  230.0 57.3 %copy-start.2 = (bf16[512,2048]{1,0:T(8,128)(2,1)S(1)}, bf16[512,2048]{1,0:T(8,128)(2,1)}, u32[]{:S(2)}) copy-start(bf16[512,2048]{1,0:T(8,128)(2,1)} %param.12) | copy-start | bytes 6291460
  287.3 9.9 %copy-start.1 = (bf16[4,16,2048]{2,1,0:T(8,128)(2,1)S(1)}, bf16[4,16,2048]{2,1,0:T(8,128)(2,1)}, u32[]{:S(2)}) copy-start(bf16[4,16,2048]{2,1,0:T(8,128)(2,1)} %param.19) | copy-start | bytes 786436
Sparse Core Ops, SparseCore 0:
  10.3 105.3 all-gather.3
  118.9 97.9 all-gather.5
  220.0 67.2 all-gather.7
where the time goes:
time: 305 us; the launch traced here: 304 us
  waiting for transfers between devices  161 us (53%)
  matrix products  66.9 us (22%)
  local copies, waits for them, and re-layouts  31 us (10%)
  starting transfers between devices  19.4 us (6%)
  between operations  13.2 us (4%)
  other arithmetic  12 us (4%)
    all_to_all x1, waiting for transfers between devices, local(): lax.all_to_all(outgoing, 'mp', split_axis=0, concat_axis=0, tiled=True)  61.8 us
    all_to_all x1, waiting for transfers between devices, local(): lax.all_to_all(value_update.astype(jnp.bfloat16), 'mp', split_axis=0, con...  53.5 us
    all_gather x1, waiting for transfers between devices, local(): lax.all_gather(value_weight, ('dp', 'mp'), axis=0, tiled=True)  27 us
    dot_general x16, matrix products, one_head(): jnp.dot(weight.astype(jnp.bfloat16), value_one, preferred_element_type=jn...  20.4 us
    all_gather x1, waiting for transfers between devices, local(): lax.all_gather(output_weight, ('dp', 'mp'), axis=0, tiled=True)  16.7 us
    dynamic_update_slice x32, local copies, waits for them, and re-layouts, taylor_heads(): outputs = lax.map(one_head, (queries, key_rows, value_rows))  12.5 us
    dot_general x1, matrix products, local(): jnp.dot(inputs, lax.all_gather(output_weight, ('dp', 'mp'), axis=0, tiled...  9.94 us
    dot_general x1, matrix products, local(): jnp.dot(inputs, lax.all_gather(value_weight, ('dp', 'mp'), axis=0, tiled=...  8.73 us
  transfers between devices with their start and end apart: 6, of which 4 were waited for; matrix products, arithmetic and copies ran while one was open for 33% of the time, Pallas kernels for 0%

commit v1 on v0

v1 whole, which is shorter than its diff:
```python
import heapq
import math

import jax
import jax.numpy as jnp
from jax import lax
from jax.experimental import pallas as pl
from jax.experimental.pallas import tpu as pltpu
from jax.sharding import PartitionSpec as P

MESH = pl.DeviceIdType.MESH

HEADS = 16
QK = 16


adapter_scale = 2.0
norm_eps = 1e-05


def prompt_index(lengths, total_token_count):
    bounds = jnp.cumsum(lengths)
    position = jnp.arange(total_token_count, dtype=jnp.int32)
    return jnp.sum((position[:, None] >= bounds[None, :]).astype(jnp.int32), axis=1)


def short_conv(value_matrix, tap_table, segment):
    result = tap_table[0][None, :] * value_matrix
    for offset in range(1, tap_table.shape[0]):
        earlier = jnp.concatenate(
            [jnp.zeros((offset, value_matrix.shape[1]), jnp.float32), value_matrix[:-offset]],
            axis=0,
        )
        same_prompt = jnp.concatenate(
            [jnp.zeros((offset,), jnp.bool_), segment[offset:] == segment[:-offset]], axis=0
        )
        result = result + tap_table[offset][None, :] * jnp.where(same_prompt[:, None], earlier, 0.0)
    return result


def taylor_heads(query_key, mixed, segment, head_count, feature):
    total_token_count, hidden_width = mixed.shape
    head_width = hidden_width // head_count
    queries = (
        query_key[:, : head_count * feature]
        .reshape(total_token_count, head_count, feature)
        .transpose(1, 0, 2)
    )
    key_rows = (
        query_key[:, head_count * feature :]
        .reshape(total_token_count, head_count, feature)
        .transpose(1, 0, 2)
    )
    value_rows = mixed.reshape(total_token_count, head_count, head_width).transpose(1, 0, 2)
    position = jnp.arange(total_token_count, dtype=jnp.int32)
    allowed = (position[None, :] <= position[:, None]) & (segment[None, :] == segment[:, None])
    score_scale = 1.0 / math.sqrt(feature)

    def one_head(operands):
        query_one, key_one, value_one = operands
        scores = jnp.dot(query_one, key_one.T, preferred_element_type=jnp.float32) * score_scale
        weight = jnp.where(allowed, 1.0 + scores + 0.5 * scores * scores, 0.0)
        row_total = jnp.sum(weight, axis=1, keepdims=True)
        numerator = jnp.dot(
            weight.astype(jnp.bfloat16), value_one, preferred_element_type=jnp.float32
        )
        return numerator / row_total

    outputs = lax.map(one_head, (queries, key_rows, value_rows))
    return outputs.transpose(1, 0, 2).reshape(total_token_count, hidden_width).astype(jnp.bfloat16)


ORDERS = ("xyz", "yzx", "zxy")
T = 128
EV = 16
SUBS = ((0, 0, (6, 5, 5)), (1, 0, (4, 4, 4)), (1, 12, (2, 3, 3)), (2, 0, (3, 3, 2)), (2, 8, (3, 2, 3)))


def size(sub_tiles, p, e):
    t = sub_tiles[p]*4096
    if e < 3: return t
    if e < 5: return 4*t
    if e < 7: return 2*t
    if e < 9: return 16*t
    if e < 11: return 8*t
    if e < 14: return 16*t
    return 8*t
def link(s, p, e):
    a1,a2,a3 = ORDERS[p]
    if e>=11: return "d"
    if e<3:
        if e==2: return a1+("+" if (s+p)%2==0 else "-")
        return a1+"+-"[e]
    if e<7: return a2+("+-+-")[e-3]
    return a3+("+-+-")[e-7]
def greedy(subs, rate=48e3, d2d=480e3, lat=1.6, depth=4.0, early=2):
    free = {}; arr = {}; heap = []; seq=0; order=[]; got=set(); pend=[]
    known=set()
    def rank(k):
        s,p,e=k
        return (s - (early if e<7 else 0), e, p)
    def want(k):
        if k not in known: known.add(k); pend.append(k)
    def flush(t):
        nonlocal seq
        pend.sort(key=rank)
        for k in list(pend):
            s,p,e=k; l=link(*k)
            if l!="d" and free.get(l,0)-t > depth: continue
            pend.remove(k)
            order.append(("send",)+k)
            r = d2d if e>=11 else rate
            st=max(t,free.get(l,0)); fin=st+size(subs[s],p,e)/r
            free[l]=fin
            heapq.heappush(heap,(fin+lat, seq, k)); seq+=1
    for s in range(len(subs)):
        for p in range(3):
            for e in (0,1): want((s,p,e))
    flush(0)
    while heap:
        t,_,k = heapq.heappop(heap); s,p,e=k
        arr[k]=t; got.add(k)
        order.append(("recv",)+k)
        g=lambda *es: all((s,p,x) in got for x in es)
        plus=(s+p)%2==0
        if e==0 and plus or e==1 and not plus: want((s,p,2))
        if g(0,1,2): want((s,p,3)); want((s,p,4))
        if e==3: want((s,p,5))
        if e==4: want((s,p,6))
        if g(0,1,2,3,4,5,6): want((s,p,7)); want((s,p,8)); want((s,p,11))
        if e==7: want((s,p,9)); want((s,p,12))
        if e==8: want((s,p,10)); want((s,p,13))
        if e==9: want((s,p,14))
        if e==10: want((s,p,15))
        flush(t)
    assert not pend
    n=len(subs)*3*16
    assert len(order)==2*n, (len(order),n)
    return order, arr, free


def cols_of(s, p):
    b, first, tiles = SUBS[s]
    start = first + sum(tiles[:p])
    return b, slice(start * T, (start + tiles[p]) * T)

def make_comm(bufs, send_sem, recv_sem):
    dp, mp = lax.axis_index("dp"), lax.axis_index("mp")
    me = {"x": mp % 4, "y": mp // 4, "z": dp // 2}
    core = dp % 2
    def device(axis, step):
        pos = dict(me)
        pos[axis] = (me[axis] + step) % 4
        return (pos["z"] * 2 + core, pos["y"] * 4 + pos["x"])
    partner = (me["z"] * 2 + 1 - core, mp)
    def region(s, p, spec, c):
        b, cols = cols_of(s, p)
        return bufs[b].at[spec["z"], c, spec["y"], spec["x"], :, cols]
    ALL, LOW, HIGH = slice(0, 4), slice(0, 2), slice(2, 4)
    def event(s, p, e):
        a1, a2, a3 = ORDERS[p]
        def reg(v1, v2, v3):
            return {a1: v1, a2: v2, a3: v3}
        def at(axis, step):
            return (me[axis] + step) % 4
        own = core
        if e < 3:
            fwd_plus = (s + p) % 2 == 0
            table = [
                (reg(me[a1], me[a2], me[a3]), reg(at(a1, -1), me[a2], me[a3]), device(a1, 1)),
                (reg(me[a1], me[a2], me[a3]), reg(at(a1, 1), me[a2], me[a3]), device(a1, -1)),
                (reg(at(a1, -1), me[a2], me[a3]), reg(at(a1, 2), me[a2], me[a3]), device(a1, 1)) if fwd_plus else
                (reg(at(a1, 1), me[a2], me[a3]), reg(at(a1, 2), me[a2], me[a3]), device(a1, -1)),
            ]
            sent, got, target = table[e]
        elif e < 7:
            table = [
                (reg(ALL, me[a2], me[a3]), reg(ALL, at(a2, -1), me[a3]), device(a2, 1)),
                (reg(ALL, me[a2], me[a3]), reg(ALL, at(a2, 1), me[a3]), device(a2, -1)),
                (reg(LOW, at(a2, -1), me[a3]), reg(LOW, at(a2, 2), me[a3]), device(a2, 1)),
                (reg(HIGH, at(a2, 1), me[a3]), reg(HIGH, at(a2, 2), me[a3]), device(a2, -1)),
            ]
            sent, got, target = table[e - 3]
        elif e < 11:
            table = [
                (reg(ALL, ALL, me[a3]), reg(ALL, ALL, at(a3, -1)), device(a3, 1)),
                (reg(ALL, ALL, me[a3]), reg(ALL, ALL, at(a3, 1)), device(a3, -1)),
                (reg(LOW, ALL, at(a3, -1)), reg(LOW, ALL, at(a3, 2)), device(a3, 1)),
                (reg(HIGH, ALL, at(a3, 1)), reg(HIGH, ALL, at(a3, 2)), device(a3, -1)),
            ]
            sent, got, target = table[e - 7]
        else:
            table = [reg(ALL, ALL, me[a3]), reg(ALL, ALL, at(a3, -1)), reg(ALL, ALL, at(a3, 1)), reg(LOW, ALL, at(a3, 2)), reg(HIGH, ALL, at(a3, 2))]
            return region(s, p, table[e - 11], core), region(s, p, table[e - 11], 1 - core), partner
        return region(s, p, sent, own), region(s, p, got, own), target
    def copy(s, p, e, received):
        sent, got, target = event(s, p, e)
        k = (s * 3 + p) * EV + e
        r = got if received else sent
        return pltpu.make_async_remote_copy(src_ref=r, dst_ref=r, send_sem=send_sem.at[k], recv_sem=recv_sem.at[k], device_id=target, device_id_type=MESH)
    def send(s, p, e):
        copy(s, p, e, False).start()
    def recv(s, p, e):
        copy(s, p, e, True).wait_recv()
    def finish():
        for s in range(len(SUBS)):
            for p in range(3):
                for e in range(EV):
                    copy(s, p, e, False).wait_send()
    def barrier():
        sem = pltpu.get_barrier_semaphore()
        for axis in "xyz":
            for d in (1, -1):
                pl.semaphore_signal(sem, inc=1, device_id=device(axis, d), device_id_type=MESH)
        pl.semaphore_signal(sem, inc=1, device_id=partner, device_id_type=MESH)
        pl.semaphore_wait(sem, 7)
    return me, core, send, recv, finish, barrier

def load_own(me, core, qk, v, o, down, up, bufs, sems):
    z, y, x = me["z"], me["y"], me["x"]
    A, V, O = bufs
    @pl.when(core == 0)
    def _(): pltpu.make_async_copy(down.at[z], A.at[z, core, y, x], sems.at[0]).start()
    @pl.when(core == 1)
    def _(): pltpu.make_async_copy(up.at[z], A.at[z, core, y, x], sems.at[0]).start()
    cs = [pltpu.make_async_copy(qk, V.at[z, core, y, x, :, 0:512], sems.at[1]),
     pltpu.make_async_copy(v, V.at[z, core, y, x, :, 512:2560], sems.at[2]),
     pltpu.make_async_copy(o, O.at[z, core, y, x], sems.at[3])]
    for c in cs: c.start()
    pltpu.make_async_copy(down.at[z], A.at[z, core, y, x], sems.at[0]).wait()
    for c in cs: c.wait()


SHAPES = ((4, 2, 4, 4, 16, 2048), (4, 2, 4, 4, 16, 2560), (4, 2, 4, 4, 16, 2048))


def gather_kernel(order, qk, v, o, down, up, out_a, out_v, out_o, buf_a, buf_v, buf_o, send_sem, recv_sem, local_sem):
    bufs = (buf_a, buf_v, buf_o)
    me, core, send, recv, finish, barrier = make_comm(bufs, send_sem, recv_sem)
    load_own(me, core, qk, v, o, down, up, bufs, local_sem)
    barrier()
    for kind, s, p, e in order:
        (send if kind == "send" else recv)(s, p, e)
    finish()
    copies = [pltpu.make_async_copy(b, t, local_sem.at[i]) for i, (b, t) in enumerate(zip(bufs, (out_a, out_v, out_o)))]
    for c in copies:
        c.start()
    for c in copies:
        c.wait()


def gather_all(qk, v, o, down, up):
    order = greedy([s[2] for s in SUBS], depth=50.0, early=0)[0]
    n = len(SUBS) * 3 * EV
    return pl.pallas_call(
        lambda *refs: gather_kernel(order, *refs),
        out_shape=[jax.ShapeDtypeStruct(s, jnp.bfloat16) for s in SHAPES],
        in_specs=[pl.BlockSpec(memory_space=pl.ANY)] * 5,
        out_specs=[pl.BlockSpec(memory_space=pl.ANY)] * 3,
        scratch_shapes=[pltpu.VMEM(s, jnp.bfloat16) for s in SHAPES]
        + [pltpu.SemaphoreType.DMA((n,)), pltpu.SemaphoreType.DMA((n,)), pltpu.SemaphoreType.DMA((4,))],
        compiler_params=pltpu.CompilerParams(collective_id=0, has_side_effects=True, vmem_limit_bytes=60 << 20),
        name="gather_all",
    )(qk, v, o, down, up)


def local(
    stream, norm_weight, query_key_weight, value_weight, output_weight, convolution_weights,
    adapter_down_maps, adapter_up_maps, prompt_lengths, block_adapter_index,
):
    adapters, qkv, out_w = gather_all(query_key_weight, value_weight, output_weight, adapter_down_maps, adapter_up_maps)
    tokens, width = stream.shape
    stream_f = stream.astype(jnp.float32)
    mean_sq = jnp.mean(stream_f * stream_f, axis=1, keepdims=True)
    normed = (stream_f * lax.rsqrt(mean_sq + norm_eps) * norm_weight[None, :]).astype(jnp.bfloat16)
    wide = jnp.dot(normed, qkv.reshape(2048, 2560), preferred_element_type=jnp.float32)
    query_key = wide[:, :512].astype(jnp.bfloat16)
    unit = (block_adapter_index % 4) * 2 * 16 + block_adapter_index // 4
    flat = adapters.reshape(128, 16, width)
    down = jnp.take(flat, unit, axis=0).reshape(256, width)
    up = jnp.take(flat, unit + 16, axis=0).reshape(256, width)
    low = lax.dot_general(normed, down, (((1,), (1,)), ((), ())), preferred_element_type=jnp.float32)
    keep = (jnp.arange(tokens) // 32)[:, None] == (jnp.arange(256) // 16)[None, :]
    low = jnp.where(keep, low, 0.0).astype(jnp.bfloat16)
    delta = adapter_scale * jnp.dot(low, up, preferred_element_type=jnp.float32)
    value_matrix = wide[:, 512:] + delta
    segment = prompt_index(prompt_lengths[0], tokens)
    conv = short_conv(value_matrix, convolution_weights, segment)
    mixed = (conv * jax.nn.silu(value_matrix)).astype(jnp.bfloat16)
    attended = taylor_heads(query_key, mixed, segment, HEADS, QK)
    projected = jnp.dot(attended, out_w.reshape(2048, 2048), preferred_element_type=jnp.float32)
    return (stream_f + projected).astype(jnp.bfloat16)


def solution(mesh):
    return jax.shard_map(
        local,
        mesh=mesh,
        in_specs=(
            P(("dp", "mp"), None),
            P(),
            P(("dp", "mp"), None),
            P(("dp", "mp"), None),
            P(("dp", "mp"), None),
            P(),
            P("mp", None, None),
            P("mp", None, None),
            P(("dp", "mp"), None),
            P(("dp", "mp")),
        ),
        out_specs=P(("dp", "mp"), None),
        check_vma=False,
    )
```

time: 305 us -> 170 us (0.56)
  waiting for transfers between devices: 161 us -> 0 us
  Pallas kernels: 0 us -> 77.5 us
  starting transfers between devices: 19.4 us -> 0 us
  between operations: 13.2 us -> 0.13 us
  matrix products: 66.9 us -> 56.7 us
  local copies, waits for them, and re-layouts: 31 us -> 22 us
    all_to_all x3 -> x0, waiting for transfers between devices: 115 us -> none  [the longest x1 61.8 us: local(): lax.all_to_all(outgoing, 'mp', split_axis=0, concat_axis=0, tiled=True)]
    pallas_call x0 -> x1, Pallas kernels: none -> 77.5 us  [gather_all(): pl.pallas_call(lambda *refs: gather_kernel(order, *refs), out_shape=[jax....]
    all_gather x3 -> x0, waiting for transfers between devices: 43.7 us -> none  [the longest x1 27 us: local(): lax.all_gather(value_weight, ('dp', 'mp'), axis=0, tiled=True)]
    all_to_all x3 -> x0, starting transfers between devices: 19.3 us -> none  [the longest x1 7.57 us: local(): lax.all_to_all(slot_local, 'mp', split_axis=0, concat_axis=0, tiled=True)]
    reshape x4 -> x0, local copies, waits for them, and re-layouts: 17.5 us -> none  [the longest x1 5.67 us: local(): returned.reshape(holders * capacity, block_rows * hidden_width)]
    dot_general x7 -> x3, matrix products: 39 us -> 28.9 us  [the longest x1 12.1 us: local(): jnp.dot(normed, qkv.reshape(2048, 2560), preferred_element_type=jnp.float32)]
    gather x0 -> x2, local copies, waits for them, and re-layouts: none -> 8.14 us  [the longest x1 4.14 us: local(): up = jnp.take(flat, unit + 16, axis=0).reshape(256, width)]
    transpose x1, other arithmetic: 4.34 us -> 8.84 us  [taylor_heads(): mixed.reshape(total_token_count, head_count, head_width).transpose(1, 0, 2)]
  transfers between devices with their start and end apart: 6 -> 0, of which waited for: 4 -> 0; matrix products, arithmetic and copies ran while one was open for 33% -> 0% of each run, Pallas kernels for 0% -> 0%
where the time goes in v1:
time: 170 us; the launch traced here: 169 us
  Pallas kernels  77.5 us (46%)
  matrix products  56.7 us (33%)
  local copies, waits for them, and re-layouts  22 us (13%)
  other arithmetic  12.9 us (8%)
    pallas_call x1, Pallas kernels, gather_all(): pl.pallas_call(lambda *refs: gather_kernel(order, *refs), out_shape=[jax....  77.5 us
    dot_general x16, matrix products, one_head(): jnp.dot(weight.astype(jnp.bfloat16), value_one, preferred_element_type=jn...  20.3 us
    dynamic_update_slice x32, local copies, waits for them, and re-layouts, taylor_heads(): outputs = lax.map(one_head, (queries, key_rows, value_rows))  12.4 us
    dot_general x1, matrix products, local(): jnp.dot(normed, qkv.reshape(2048, 2560), preferred_element_type=jnp.float32)  12.1 us
    dot_general x1, matrix products, local(): jnp.dot(attended, out_w.reshape(2048, 2048), preferred_element_type=jnp.f...  9.96 us
    transpose x1, other arithmetic, taylor_heads(): mixed.reshape(total_token_count, head_count, head_width).transpose(1, 0, 2)  8.84 us
    dot_general x16, matrix products, one_head(): jnp.dot(query_one, key_one.T, preferred_element_type=jnp.float32)  7.5 us
    dot_general x1, matrix products, local(): delta = adapter_scale * jnp.dot(low, up, preferred_element_type=jnp.float32)  6.8 us

profile of v1, /device:TPU:1, one launch (start us, length us, event | category | flops | bytes accessed | tf_op | source)
XLA Modules:
  0.0 169.4 jit_solution(5478970948987229695)
XLA Ops:
  0.0 77.5 %gather_all.1 = (bf16[4,2,4,4,16,2048]{5,4,3,2,1,0:T(8,128)(2,1)}, bf16[4,2,4,4,16,2560]{5,4,3,2,1,0:T(8,128)(2,1)}, bf16[4,2,4,4,16,2048]{5,4,3,2,1,0:T(8,128)(2,1)}) custom-call(bf16[16,512]{1,0:T(8,128)(2,1)} %refs_0_.1, bf16[16,2048]{1,0:T(8,128)(2,1)} %refs_1_.1, bf16[16,2048]{1,0:T(8,128)(2,1)} %refs_2_.1, bf16[4,16,2048]{2,1,0:T(8,128)(2,1)} %refs_3_.1, ...), custom_call_target="tpu_custom_call" | custom-call | tf_op jit(solution)/shard_map/gather_all/pallas_call | solution.py:255
  77.5 0.7 compare_and_fusion.1
  78.2 4.1 %gather_fusion.1 = bf16[16,16,2048]{2,1,0:T(8,128)(2,1)S(1)} fusion(bf16[128,16,2048]{2,1,0:T(8,128)(2,1)} %bitcast.63, s32[1024]{0:T(1024)S(1)} %pad_clamp_fusion), kind=kCustom, calls=%fused_computation.1.clone | custom fusion | bytes 2097216 | tf_op jit(solution)/shard_map/jit(_take)/gather | solution.py:281
  82.4 1.1 broadcast_select_fusion
  83.5 4.0 %gather_fusion = bf16[16,16,2048]{2,1,0:T(8,128)(2,1)S(1)} fusion(bf16[128,16,2048]{2,1,0:T(8,128)(2,1)} %bitcast.64, s32[1024]{0:T(1024)S(1)} %pad_clamp_fusion.1), kind=kCustom, calls=%fused_computation.clone | custom fusion | bytes 2097216 | tf_op jit(solution)/shard_map/jit(_take)/gather | solution.py:280
  87.5 1.2 broadcast_select_fusion.1
  88.7 0.5 fusion.13
  89.2 12.1 %fusion.37 = (bf16[512,2560]{1,0:T(8,128)(2,1)}, f32[512,2560]{1,0:T(8,128)}) fusion(bf16[2048,2560]{1,0:T(8,128)(2,1)} %bitcast.71, bf16[512,2048]{1,0:T(8,128)(2,1)S(1)} %copy-done, f32[2048]{0:T(1024)S(1)} %copy-done.3, f32[512]{0:T(512)S(1)} %add_rsqrt_fusion), kind=kOutput, calls=%fused_computation.72 | convolution fusion | flops 5374214144 | bytes 20457472 | tf_op jit(solution)/shard_map/dot_general | solution.py:276
  101.4 6.8 %slice_add_fusion = f32[512,2048]{1,0:T(8,128)} fusion(f32[512,2560]{1,0:T(8,128)} %get-tuple-element.129, bf16[256,2048]{1,0:T(8,128)(2,1)S(1)} %bitcast.61, bf16[256,2048]{1,0:T(8,128)(2,1)} %bitcast.62, bf16[512,2048]{1,0:T(8,128)(2,1)S(1)} %copy-done, f32[2048]{0:T(1024)S(1)} %copy-done.3, f32[512]{0:T(512)S(1)} %add_rsqrt_fusion, ...), kind=kOutput, calls=%fused_computation.25 | convolution fusion | flops 1080426496 | bytes 12596224 | tf_op jit(solution)/shard_map/dot_general | solution.py:285
  108.8 8.8 %bitcast_bitcast_fusion = bf16[16,512,128]{2,1,0:T(8,128)(2,1)} fusion(f32[512,2048]{1,0:T(8,128)} %slice_add_fusion, f32[510,2048]{1,0:T(8,128)} %bitcast.59, pred[512]{0:T(512)(128)(4,1)S(1)} %concatenate.14, f32[2048]{0:T(1024)S(1)} %bitcast.68, f32[511,2048]{1,0:T(8,128)} %bitcast.60, pred[512]{0:T(512)(128)(4,1)S(1)} %pad_add_fusion, ...), kind=kLoop, calls=%fused_computation.27 | loop fusion | flops 13631488 | bytes 14681088 | tf_op jit(solution)/shard_map/transpose | solution.py:54
  117.7 1.1 fusion.35
  119.0 40.4 %while.13 = (s32[]{:T(128)}, bf16[16,512,128]{1,2,0:T(8,128)(2,1)}, bf16[16,512,16]{1,2,0:T(8,128)(2,1)S(1)}, bf16[16,512,16]{1,2,0:T(8,128)(2,1)S(1)}, bf16[16,...) while((s32[]{:T(128)}, bf16[16,512,128]{1,2,0:T(8,128)(2,1)}, ...), condition=%wide.region_5.7_spmd.clone, body=%wide.region_3.6_spmd.clone.sunk | while | flops 78511616 | bytes 1878093 | solution.py:69
  119.0 0.5 fusion.51
  119.5 1.3 fusion.52
  120.9 0.6 constant_dynamic-update-slice_fusion.2
  122.0 1.3 fusion.52
  123.4 0.7 constant_dynamic-update-slice_fusion.2
  124.5 1.3 fusion.52
  125.9 0.7 constant_dynamic-update-slice_fusion.2
  127.1 1.3 fusion.52
  128.5 0.7 constant_dynamic-update-slice_fusion.2
  129.6 1.3 fusion.52
  131.0 0.7 constant_dynamic-update-slice_fusion.2
  132.1 1.3 fusion.52
  133.5 0.7 constant_dynamic-update-slice_fusion.2
  134.6 1.3 fusion.52
  136.0 0.7 constant_dynamic-update-slice_fusion.2
  137.2 1.3 fusion.52
  138.6 0.7 constant_dynamic-update-slice_fusion.2
  139.7 1.3 fusion.52
  141.1 0.7 constant_dynamic-update-slice_fusion.2
  142.2 1.3 fusion.52
  143.6 0.7 constant_dynamic-update-slice_fusion.2
  144.3 0.5 fusion.51
  144.8 1.3 fusion.52
  146.1 0.7 constant_dynamic-update-slice_fusion.2
  147.3 1.3 fusion.52
  148.7 0.7 constant_dynamic-update-slice_fusion.2
  149.8 1.3 fusion.52
  151.2 0.7 constant_dynamic-update-slice_fusion.2
  152.3 1.3 fusion.52
  153.7 0.7 constant_dynamic-update-slice_fusion.2
  154.4 0.5 fusion.51
  154.9 1.3 fusion.52
  156.3 0.7 constant_dynamic-update-slice_fusion.2
  157.4 1.3 fusion.52
  158.8 0.7 constant_dynamic-update-slice_fusion.2
  159.4 10.0 %fusion.16 = bf16[512,2048]{1,0:T(8,128)(2,1)} fusion(bf16[512,2048]{1,0:T(8,128)(2,1)S(1)} %copy-done, bf16[512,2048]{0,1:T(8,128)(2,1)} %bitcast.73, bf16[2048,2048]{1,0:T(8,128)(2,1)} %bitcast.72), kind=kOutput, calls=%fused_computation.24 | convolution fusion | flops 4298113024 | bytes 14680064 | tf_op jit(solution)/shard_map/dot_general | solution.py:291
  (56 shorter events, 8.9 us)
Async XLA Ops:
  78.2 10.5 %copy-start = (bf16[512,2048]{1,0:T(8,128)(2,1)S(1)}, bf16[512,2048]{1,0:T(8,128)(2,1)}, u32[]{:S(2)}) copy-start(bf16[512,2048]{1,0:T(8,128)(2,1)} %param.14) | copy-start | bytes 6291460
  82.4 6.8 %copy-start.3 = (f32[2048]{0:T(1024)S(1)}, f32[2048]{0:T(1024)}, u32[]{:S(2)}) copy-start(f32[2048]{0:T(1024)} %param.15) | copy-start | bytes 24580
  89.2 12.2 %copy-start.1 = (bf16[16,16,2048]{2,1,0:T(8,128)(2,1)S(1)}, bf16[16,16,2048]{2,1,0:T(8,128)(2,1)}, u32[]{:S(2)}) copy-start(bf16[16,16,2048]{2,1,0:T(8,128)(2,1)} %broadcast_select_fusion) | copy-start | bytes 3145732
  101.4 6.8 %copy-start.4 = (s32[1,8]{1,0:T(1,128)S(1)}, s32[1,8]{1,0:T(1,128)}, u32[]{:S(2)}) copy-start(s32[1,8]{1,0:T(1,128)} %param.22) | copy-start | bytes 100
  101.4 7.4 %copy-start.2 = (f32[3,2048]{1,0:T(4,128)S(1)}, f32[3,2048]{1,0:T(4,128)}, u32[]{:S(2)}) copy-start(f32[3,2048]{1,0:T(4,128)} %param.19) | copy-start | bytes 73732

commit v2 on v0

v2 whole, which is shorter than its diff:
```python
import heapq

import jax
import jax.numpy as jnp
from jax import lax
from jax.experimental import pallas as pl
from jax.experimental.pallas import tpu as pltpu
from jax.sharding import PartitionSpec as P

MESH = pl.DeviceIdType.MESH
F32, BF16 = jnp.float32, jnp.bfloat16
HEADS = 16
QK = 16
BLK = 32
NORM_EPS = 1e-05
TOK, WIDTH = 512, 2048

ORDERS = ("xyz", "yzx", "zxy")
TILE = 128
EVENTS = 16
SHAPES = ((4, 2, 4, 4, 16, WIDTH), (4, 2, 4, 4, 16, 512 + WIDTH), (4, 2, 4, 4, 16, WIDTH))
SLABS = ((1, 0, (4, 4, 4)), (1, 12, (2, 3, 3)), (0, 0, (6, 5, 5)), (2, 0, (3, 3, 2)), (2, 8, (3, 2, 3)))


def event_bytes(tiles, part, event):
    unit = tiles[part] * 16 * TILE * 2
    return unit * (1 if event < 3 else 4 if event < 5 else 2 if event < 7 else 16 if event < 9 else 8 if event < 11 else 16 if event < 14 else 8)


def event_link(slab, part, event):
    a1, a2, a3 = ORDERS[part]
    if event >= 11:
        return "d"
    if event == 2:
        return a1 + ("+" if (slab + part) % 2 == 0 else "-")
    if event < 3:
        return a1 + "+-"[event]
    if event < 7:
        return a2 + "+-+-"[event - 3]
    return a3 + "+-+-"[event - 7]


def plan(pieces, rate=48e3, partner_rate=480e3, latency=1.6, depth=4.0, early=2, t_start=0.0):
    tiles = [s[2] for s in SLABS]
    free, arrived, heap, order, got, waiting, known = {}, {}, [], [], set(), [], set()
    left = {s: 3 * EVENTS for s in range(len(SLABS))}
    todo = list(pieces)
    state = {"seq": 0}

    def rank(k):
        return (k[0] - (early if k[2] < 7 else 0), k[2], k[1])

    def want(s, p, *events):
        for e in events:
            if (s, p, e) not in known:
                known.add((s, p, e))
                waiting.append((s, p, e))

    def flush(t):
        waiting.sort(key=rank)
        for k in list(waiting):
            link = event_link(*k)
            if link != "d" and free.get(link, 0) - t > depth:
                continue
            waiting.remove(k)
            order.append(("send",) + k)
            start = max(t, free.get(link, 0))
            end = start + event_bytes(tiles[k[0]], k[1], k[2]) / (partner_rate if k[2] >= 11 else rate)
            free[link] = end
            heapq.heappush(heap, (end + latency, state["seq"], k))
            state["seq"] += 1

    def arrive(k):
        s, p, e = k
        got.add(k)
        left[s] -= 1
        order.append(("recv",) + k)
        have = lambda *events: all((s, p, x) in got for x in events)
        if e == (0 if (s + p) % 2 == 0 else 1):
            want(s, p, 2)
        if have(0, 1, 2):
            want(s, p, 3, 4)
        if e == 3:
            want(s, p, 5)
        if e == 4:
            want(s, p, 6)
        if have(0, 1, 2, 3, 4, 5, 6):
            want(s, p, 7, 8, 11)
        if e == 7:
            want(s, p, 9, 12)
        if e == 8:
            want(s, p, 10, 13)
        if e == 9:
            want(s, p, 14)
        if e == 10:
            want(s, p, 15)

    for s in range(len(SLABS)):
        for p in range(3):
            want(s, p, 0, 1)
    t = t_start
    log = []
    while heap or waiting or todo:
        while heap and heap[0][0] <= t:
            arrive(heapq.heappop(heap)[2])
        flush(t)
        ready = [c for c in todo[:1] if all(left[s] == 0 for s in c[1])]
        if ready:
            todo.remove(ready[0])
            order.append(("run", ready[0][0]))
            log.append((round(t, 1), ready[0][0]))
            t += ready[0][2]
        elif heap:
            t = max(t, heap[0][0])
    return order, t, log


def columns_of(slab, part):
    buf, first, tiles = SLABS[slab]
    start = first + sum(tiles[:part])
    return buf, slice(start * TILE, (start + tiles[part]) * TILE)


def make_comm(bufs, send_sem, recv_sem):
    dp, mp = lax.axis_index("dp"), lax.axis_index("mp")
    me = {"x": mp % 4, "y": mp // 4, "z": dp // 2}
    core = dp % 2
    partner = (me["z"] * 2 + 1 - core, mp)
    every, low, high = slice(0, 4), slice(0, 2), slice(2, 4)

    def at(axis, step):
        return (me[axis] + step) % 4

    def device(axis, step):
        pos = dict(me)
        pos[axis] = at(axis, step)
        return (pos["z"] * 2 + core, pos["y"] * 4 + pos["x"])

    def region(slab, part, pos, which_core):
        buf, cols = columns_of(slab, part)
        return bufs[buf].at[pos["z"], which_core, pos["y"], pos["x"], :, cols]

    def event(slab, part, e):
        a1, a2, a3 = ORDERS[part]

        def pos(v1, v2, v3):
            return {a1: v1, a2: v2, a3: v3}

        if e < 2:
            step = 1 if e == 0 else -1
            sent, got, target = pos(me[a1], me[a2], me[a3]), pos(at(a1, -step), me[a2], me[a3]), device(a1, step)
        elif e == 2:
            step = 1 if (slab + part) % 2 == 0 else -1
            sent, got, target = pos(at(a1, -step), me[a2], me[a3]), pos(at(a1, 2), me[a2], me[a3]), device(a1, step)
        elif e < 5:
            step = 1 if e == 3 else -1
            sent, got, target = pos(every, me[a2], me[a3]), pos(every, at(a2, -step), me[a3]), device(a2, step)
        elif e < 7:
            step, half = (1, low) if e == 5 else (-1, high)
            sent, got, target = pos(half, at(a2, -step), me[a3]), pos(half, at(a2, 2), me[a3]), device(a2, step)
        elif e < 9:
            step = 1 if e == 7 else -1
            sent, got, target = pos(every, every, me[a3]), pos(every, every, at(a3, -step)), device(a3, step)
        elif e < 11:
            step, half = (1, low) if e == 9 else (-1, high)
            sent, got, target = pos(half, every, at(a3, -step)), pos(half, every, at(a3, 2)), device(a3, step)
        else:
            step, half = ((0, every), (-1, every), (1, every), (2, low), (2, high))[e - 11]
            where = pos(half, every, at(a3, step))
            return region(slab, part, where, core), region(slab, part, where, 1 - core), partner
        return region(slab, part, sent, core), region(slab, part, got, core), target

    def copy(slab, part, e, received):
        sent, got, target = event(slab, part, e)
        k = (slab * 3 + part) * EVENTS + e
        ref = got if received else sent
        return pltpu.make_async_remote_copy(
            src_ref=ref, dst_ref=ref, send_sem=send_sem.at[k], recv_sem=recv_sem.at[k],
            device_id=target, device_id_type=MESH,
        )

    def send(slab, part, e):
        copy(slab, part, e, False).start()

    def recv(slab, part, e):
        copy(slab, part, e, True).wait_recv()

    def finish():
        for slab in range(len(SLABS)):
            for part in range(3):
                for e in range(EVENTS):
                    copy(slab, part, e, False).wait_send()

    def barrier():
        sem = pltpu.get_barrier_semaphore()
        for axis in "xyz":
            for step in (1, -1):
                pl.semaphore_signal(sem, inc=1, device_id=device(axis, step), device_id_type=MESH)
        pl.semaphore_signal(sem, inc=1, device_id=partner, device_id_type=MESH)
        pl.semaphore_wait(sem, 7)

    return me, core, send, recv, finish, barrier


def own_copies(me, core, qk, v, o, down, up, bufs, sems):
    z, y, x = me["z"], me["y"], me["x"]
    a_buf, v_buf, o_buf = bufs
    adapter = a_buf.at[z, core, y, x]

    @pl.when(core == 0)
    def _():
        pltpu.make_async_copy(down.at[z], adapter, sems.at[0]).start()

    @pl.when(core == 1)
    def _():
        pltpu.make_async_copy(up.at[z], adapter, sems.at[0]).start()

    copies = [
        pltpu.make_async_copy(qk, v_buf.at[z, core, y, x, :, 0:512], sems.at[1]),
        pltpu.make_async_copy(v, v_buf.at[z, core, y, x, :, 512 : 512 + WIDTH], sems.at[2]),
        pltpu.make_async_copy(o, o_buf.at[z, core, y, x], sems.at[3]),
    ]
    for c in copies:
        c.start()

    def wait():
        pltpu.make_async_copy(down.at[z], adapter, sems.at[0]).wait()
        for c in copies:
            c.wait()

    return wait


def dot(a, b):
    return jnp.dot(a, b, preferred_element_type=F32)


def dot_t(a, b):
    return lax.dot_general(a, b, (((1,), (1,)), ((), ())), preferred_element_type=F32)


def kernel(
    order, lengths, adapters, stream, gain, qk, v, o, taps, down, up, out,
    a_buf, v_buf, o_buf, x_buf, normed, values, qk_buf, attended, sel_down, sel_up, low_buf, mix, mask, same,
    send_sem, recv_sem, local_sem,
):
    bufs = (a_buf, v_buf, o_buf)
    me, core, send, recv, finish, barrier = make_comm(bufs, send_sem, recv_sem)
    wait_own = own_copies(me, core, qk, v, o, down, up, bufs, local_sem)
    stream_in = pltpu.make_async_copy(stream, x_buf, local_sem.at[4])
    stream_in.start()
    wait_own()
    barrier()

    def tile(buf, start, width):
        cols = pl.ds(pl.multiple_of(start, 128), width)
        return buf[:, :, :, :, :, cols].reshape(2048, width)

    def norm():
        stream_in.wait()

        def rows(i, _):
            r = pl.ds(pl.multiple_of(i * 32, 32), 32)
            x = x_buf[r, :].astype(F32)
            mean_sq = jnp.mean(x * x, axis=1, keepdims=True)
            normed[r, :] = (x * lax.rsqrt(mean_sq + NORM_EPS) * gain[...]).astype(BF16)
            return 0

        lax.fori_loop(0, TOK // 32, rows, 0)

    def masks():
        bounds, total = [], 0
        for k in range(8):
            total = total + lengths[0, k]
            bounds.append(total)

        def rows(i, _):
            r = pl.ds(pl.multiple_of(i * 64, 64), 64)

            def start_of(width):
                t = lax.broadcasted_iota(jnp.int32, (64, width), 0) + i * 64
                first = jnp.zeros((64, width), jnp.int32)
                for b in bounds:
                    first = jnp.where(t >= b, b, first)
                return t, first

            t, first = start_of(512)
            s = lax.broadcasted_iota(jnp.int32, (64, 512), 1)
            mask[r, :] = jnp.where((s <= t) & (s >= first), 0.5, 0.0).astype(F32)
            t, first = start_of(128)
            same[0, r, :] = jnp.where(t - 1 >= first, 1.0, 0.0).astype(F32)
            same[1, r, :] = jnp.where(t - 2 >= first, 1.0, 0.0).astype(F32)
            return 0

        lax.fori_loop(0, TOK // 64, rows, 0)

    def project_qk():
        def one(i, _):
            c = pl.ds(pl.multiple_of(i * 256, 256), 256)
            qk_buf[:, c] = dot(normed[...], tile(v_buf, i * 256, 256)).astype(BF16)
            return 0

        lax.fori_loop(0, 2, one, 0)

    def project_v(first, count):
        def one(i, _):
            c = pl.ds(pl.multiple_of(i * 256, 256), 256)
            values[:, c] = dot(normed[...], tile(v_buf, 512 + i * 256, 256))
            return 0

        lax.fori_loop(first, first + count, one, 0)

    def low_rank():
        for b in range(TOK // BLK):
            a = adapters[b]
            z, m = lax.rem(a, 4), lax.div(a, 4)
            y, x = lax.div(m, 4), lax.rem(m, 4)
            sel_down[b * 16 : (b + 1) * 16, :] = a_buf[z, 0, y, x]
            sel_up[b * 16 : (b + 1) * 16, :] = a_buf[z, 1, y, x]
        low = dot_t(normed[...], sel_down[...])
        block = lax.broadcasted_iota(jnp.int32, (TOK, 256), 0) // BLK
        owner = lax.broadcasted_iota(jnp.int32, (TOK, 256), 1) // 16
        low_buf[...] = (2.0 * jnp.where(block == owner, low, 0.0)).astype(BF16)

    def heads(first, count):
        def one(h, _):
            c = pl.ds(pl.multiple_of(h * 128, 128), 128)
            val = values[:, c] + dot(low_buf[...], sel_up[:, c]).astype(BF16).astype(F32)
            conv = taps[0:1, c] * val
            conv = conv + taps[1:2, c] * (pltpu.roll(val, 1, axis=0) * same[0])
            conv = conv + taps[2:3, c] * (pltpu.roll(val, 2, axis=0) * same[1])
            mix[...] = (conv * (val / (1.0 + jnp.exp(-val)))).astype(BF16)
            group = pl.multiple_of(h // 8 * 128, 128)
            lane_head = lax.broadcasted_iota(jnp.int32, (TOK, 128), 1) // 16
            q = qk_buf[:, pl.ds(group, 128)].astype(F32)
            q = jnp.where(lane_head == h % 8, q * 0.25, 0.0).astype(BF16)
            k = qk_buf[:, pl.ds(256 + group, 128)]
            for r0, k0, k1 in ((0, 0, 128), (128, 0, 256), (256, 0, 384), (384, 128, 512)):
                u1 = dot_t(q[r0 : r0 + 128], k[k0:k1]) + 1.0
                weight = ((u1 * u1 + 1.0) * mask[r0 : r0 + 128, k0:k1]).astype(BF16)
                right = jnp.concatenate([mix[k0:k1, :], jnp.ones((k1 - k0, 128), BF16)], axis=1)
                both = dot(weight, right)
                attended[r0 : r0 + 128, c] = (both[:, :128] / both[:, 128:]).astype(BF16)
            return 0

        lax.fori_loop(first, first + count, one, 0)

    out_copies = []

    def project_out(first, count):
        def one(i, _):
            c = pl.ds(pl.multiple_of(i * 256, 256), 256)
            x_buf[:, c] = (x_buf[:, c].astype(F32) + dot(attended[...], tile(o_buf, i * 256, 256))).astype(BF16)
            return 0

        lax.fori_loop(first, first + count, one, 0)
        c = slice(first * 256, (first + count) * 256)
        done = pltpu.make_async_copy(x_buf.at[:, c], out.at[:, c], local_sem.at[5 + len(out_copies)])
        done.start()
        out_copies.append(done)

    run = {"norm": norm, "masks": masks, "qk": project_qk, "low": low_rank}
    for op in order:
        if op[0] == "send":
            send(*op[1:])
        elif op[0] == "recv":
            recv(*op[1:])
        elif op[1] in run:
            run[op[1]]()
        else:
            {"v": project_v, "h": heads, "o": project_out}[op[1][0]](*op[1][1:])
    finish()
    for c in out_copies:
        c.wait()


PIECES = [
    ("norm", (), 2.0),
    ("masks", (), 0.7),
    ("qk", (0,), 1.6),
    (("v", 0, 2), (0,), 1.6),
    (("v", 2, 2), (0,), 1.6),
    (("v", 4, 2), (1,), 1.6),
    (("v", 6, 2), (1,), 1.6),
    ("low", (2,), 2.0),
    (("h", 0, 4), (), 3.0),
    (("h", 4, 4), (), 3.0),
    (("h", 8, 4), (), 3.0),
    (("h", 12, 4), (), 3.0),
    (("o", 0, 4), (3,), 3.2),
    (("o", 4, 4), (4,), 3.2),
]


def local(
    stream, norm_weight, query_key_weight, value_weight, output_weight, convolution_weights,
    adapter_down_maps, adapter_up_maps, prompt_lengths, block_adapter_index,
):
    order = plan(PIECES)[0]
    n = len(SLABS) * 3 * EVENTS
    any_, smem, vmem = (pl.BlockSpec(memory_space=m) for m in (pl.ANY, pltpu.SMEM, pltpu.VMEM))
    return pl.pallas_call(
        lambda *refs: kernel(order, *refs),
        out_shape=jax.ShapeDtypeStruct((TOK, WIDTH), BF16),
        in_specs=[smem, smem, any_, vmem, any_, any_, any_, vmem, any_, any_],
        out_specs=any_,
        scratch_shapes=[pltpu.VMEM(s, BF16) for s in SHAPES]
        + [
            pltpu.VMEM((TOK, WIDTH), BF16),
            pltpu.VMEM((TOK, WIDTH), BF16),
            pltpu.VMEM((TOK, WIDTH), F32),
            pltpu.VMEM((TOK, 512), BF16),
            pltpu.VMEM((TOK, WIDTH), BF16),
            pltpu.VMEM((256, WIDTH), BF16),
            pltpu.VMEM((256, WIDTH), BF16),
            pltpu.VMEM((TOK, 256), BF16),
            pltpu.VMEM((TOK, 128), BF16),
            pltpu.VMEM((TOK, TOK), F32),
            pltpu.VMEM((2, TOK, 128), F32),
            pltpu.SemaphoreType.DMA((n,)),
            pltpu.SemaphoreType.DMA((n,)),
            pltpu.SemaphoreType.DMA((16,)),
        ],
        compiler_params=pltpu.CompilerParams(
            collective_id=0, has_side_effects=True, vmem_limit_bytes=62 << 20
        ),
        name="layer",
    )(
        prompt_lengths, block_adapter_index, stream, norm_weight.reshape(1, WIDTH), query_key_weight,
        value_weight, output_weight, convolution_weights, adapter_down_maps, adapter_up_maps,
    )


def solution(mesh):
    rows, whole = P(("dp", "mp"), None), P()
    return jax.shard_map(
        local,
        mesh=mesh,
        in_specs=(
            rows, whole, rows, rows, rows, whole, P("mp", None, None), P("mp", None, None), rows, P(("dp", "mp")),
        ),
        out_specs=rows,
        check_vma=False,
    )
```

time: 305 us -> 91.5 us (0.30)
  waiting for transfers between devices: 161 us -> 0 us
  Pallas kernels: 0 us -> 88.1 us
  matrix products: 66.9 us -> 0 us
  local copies, waits for them, and re-layouts: 31 us -> 3.16 us
  starting transfers between devices: 19.4 us -> 0 us
  between operations: 13.2 us -> 0.01 us
  other arithmetic: 12 us -> 0 us
    all_to_all x3 -> x0, waiting for transfers between devices: 115 us -> none  [the longest x1 61.8 us: local(): lax.all_to_all(outgoing, 'mp', split_axis=0, concat_axis=0, tiled=True)]
    pallas_call x0 -> x1, Pallas kernels: none -> 88.1 us  [local(): pl.pallas_call(lambda *refs: kernel(order, *refs), out_shape=jax.ShapeDty...]
    dot_general x39 -> x0, matrix products: 66.9 us -> none  [the longest x16 20.4 us: one_head(): jnp.dot(weight.astype(jnp.bfloat16), value_one, preferred_element_type=jn...]
    all_gather x3 -> x0, waiting for transfers between devices: 43.7 us -> none  [the longest x1 27 us: local(): lax.all_gather(value_weight, ('dp', 'mp'), axis=0, tiled=True)]
    all_to_all x3 -> x0, starting transfers between devices: 19.3 us -> none  [the longest x1 7.57 us: local(): lax.all_to_all(slot_local, 'mp', split_axis=0, concat_axis=0, tiled=True)]
    reshape x4 -> x0, local copies, waits for them, and re-layouts: 17.5 us -> none  [the longest x1 5.67 us: local(): returned.reshape(holders * capacity, block_rows * hidden_width)]
    dynamic_update_slice x32 -> x0, local copies, waits for them, and re-layouts: 12.5 us -> none  [taylor_heads(): outputs = lax.map(one_head, (queries, key_rows, value_rows))]
    transpose x1 -> x0, other arithmetic: 4.34 us -> none  [taylor_heads(): mixed.reshape(total_token_count, head_count, head_width).transpose(1, 0, 2)]
  transfers between devices with their start and end apart: 6 -> 0, of which waited for: 4 -> 0; matrix products, arithmetic and copies ran while one was open for 33% -> 0% of each run, Pallas kernels for 0% -> 0%
where the time goes in v2:
time: 91.5 us; the launch traced here: 91.2 us
  Pallas kernels  88.1 us (96%)
  local copies, waits for them, and re-layouts  3.16 us (3%)
    pallas_call x1, Pallas kernels, local(): pl.pallas_call(lambda *refs: kernel(order, *refs), out_shape=jax.ShapeDty...  88.1 us
    unnamed x1, local copies, waits for them, and re-layouts  3.16 us

profile of v2, /device:TPU:1, one launch (start us, length us, event | category | flops | bytes accessed | tf_op | source)
XLA Modules:
  0.0 91.2 jit_solution(15910533738382584180)
XLA Ops:
  0.0 88.1 %layer.1 = bf16[512,2048]{1,0:T(8,128)(2,1)} custom-call(s32[1,8]{1,0:T(1,128)} %refs_0_.1, s32[16]{0:T(128)} %refs_1_.1, bf16[512,2048]{1,0:T(8,128)(2,1)} %refs_2_.1, f32[1,2048]{1,0:T(1,128)} %bitcast.1, bf16[16,512]{1,0:T(8,128)(2,1)} %refs_4_.1, bf16[16,2048]{1,0:T(8,128)(2,1)} %refs_5_.1, bf16[16,2048]{1,0:T(8,128)(2,1)} %refs_6_.1, ...), custom_call_target="tpu_custom_call" | custom-call | tf_op jit(solution)/shard_map/layer/pallas_call | solution.py:402
  88.1 3.2 %copy.12 = bf16[512,2048]{1,0:T(8,128)(2,1)} copy(bf16[512,2048]{1,0:T(8,128)(2,1)} %layer.1) | data formatting | bytes 4194304

commit v3 on v2

v3 whole, which is shorter than its diff:
```python
import heapq

import jax
import jax.numpy as jnp
from jax import lax
from jax.experimental import pallas as pl
from jax.experimental.pallas import tpu as pltpu
from jax.sharding import PartitionSpec as P

MESH = pl.DeviceIdType.MESH
F32, BF16 = jnp.float32, jnp.bfloat16
HEADS = 16
QK = 16
BLK = 32
NORM_EPS = 1e-05
TOK, WIDTH = 512, 2048

ORDERS = ("xyz", "yzx", "zxy")
TILE = 128


def make_events(fine):
    ev = [(1, 1, (0, 0, 0), ()), (1, -1, (0, 0, 0), ())]
    ev.append((1, 1, (-1, 0, 0), (0,)))
    if fine:
        first = {0: (), -1: (0,), 1: (1,), 2: (2,)}
        second = {0: [0, 1, 2], -1: [], 1: [], 2: []}
        for a in (0, -1, 1, 2):
            n = len(ev)
            ev.append((2, 1, (a, 0, 0), first[a]))
            ev.append((2, -1, (a, 0, 0), first[a]))
            step = 1 if a in (0, -1) else -1
            ev.append((2, step, (a, -step, 0), (n if step == 1 else n + 1,)))
            second[-1].append(n)
            second[1].append(n + 1)
            second[2].append(n + 2)
        third = {0: [0, 1, 2] + second[-1] + second[1] + second[2], -1: [], 1: [], 2: []}
        for b in (0, -1, 1, 2):
            n = len(ev)
            ev.append((3, 1, ("all", b, 0), tuple(second[b])))
            ev.append((3, -1, ("all", b, 0), tuple(second[b])))
            step = 1 if b in (0, -1) else -1
            ev.append((3, step, ("all", b, -step), (n if step == 1 else n + 1,)))
            third[-1].append(n)
            third[1].append(n + 1)
            third[2].append(n + 2)
        for c in (0, -1, 1, 2):
            ev.append((4, 0, ("all", "all", c), tuple(third[c])))
    else:
        ev.append((2, 1, ("all", 0, 0), (0, 1, 2)))
        ev.append((2, -1, ("all", 0, 0), (0, 1, 2)))
        ev.append((2, 1, ("low", -1, 0), (3,)))
        ev.append((2, -1, ("high", 1, 0), (4,)))
        stage2 = (0, 1, 2, 3, 4, 5, 6)
        ev.append((3, 1, ("low", "all", 0), stage2))
        ev.append((3, -1, ("high", "all", 0), stage2))
        ev.append((3, 1, ("high", "all", 0), stage2))
        ev.append((3, -1, ("low", "all", 0), stage2))
        ev.append((3, 1, ("low", "all", -1), (7,)))
        ev.append((3, -1, ("high", "all", 1), (8,)))
        ev.append((4, 0, ("all", "all", 0), stage2))
        ev.append((4, 0, ("all", "all", -1), (7, 9)))
        ev.append((4, 0, ("all", "all", 1), (8, 10)))
        ev.append((4, 0, ("low", "all", 2), (11,)))
        ev.append((4, 0, ("high", "all", 2), (12,)))
    return ev


EV = make_events(False)
EVENTS = len(EV)


def event_of(slab, part, e):
    stage, step, spec, needs = EV[e]
    if e == 2 and (slab + part) % 2:
        return 1, -1, (1, 0, 0), (1,)
    return stage, step, spec, needs


SHAPES = ((4, 2, 4, 4, 16, WIDTH), (4, 2, 4, 4, 16, 512 + WIDTH), (4, 2, 4, 4, 16, WIDTH))
SLABS = ((1, 0, (4, 4, 4)), (1, 12, (2, 3, 3)), (0, 0, (6, 5, 5)), (2, 0, (3, 3, 2)), (2, 8, (3, 2, 3)))


def event_bytes(slab, part, e):
    units = 1
    for s in event_of(slab, part, e)[2]:
        units *= {"all": 4, "low": 2, "high": 2}.get(s, 1)
    return units * SLABS[slab][2][part] * 16 * TILE * 2


def plan(pieces, rate=46e3, partner_rate=480e3, latency=1.8, depth=2.0, early=1):
    free, heap, order, log = {}, [], [], []
    got = [[set() for _ in range(3)] for _ in SLABS]
    waiting = [(s, p, e) for s in range(len(SLABS)) for p in range(3) for e in range(EVENTS)]
    waiting.sort(key=lambda k: (k[0] - (0, early, early, 0, 0)[EV[k[2]][0]], EV[k[2]][0], k[2], k[1]))
    todo = list(pieces)
    seq, t = 0, 0.0
    while heap or waiting or todo:
        while heap and heap[0][0] <= t:
            s, p, e = heapq.heappop(heap)[2]
            got[s][p].add(e)
            order.append(("recv", s, p, e))
        for k in list(waiting):
            s, p, e = k
            stage, step, _, needs = event_of(s, p, e)
            link = (ORDERS[p][stage - 1], step) if stage < 4 else "partner"
            if not all(n in got[s][p] for n in needs) or (stage < 4 and free.get(link, 0) - t > depth):
                continue
            waiting.remove(k)
            order.append(("send",) + k)
            end = max(t, free.get(link, 0)) + event_bytes(s, p, e) / (rate if stage < 4 else partner_rate)
            free[link] = end
            heapq.heappush(heap, (end + latency, seq, k))
            seq += 1
        if todo and all(len(got[s][p]) == EVENTS for s in todo[0][1] for p in range(3)):
            name, _, cost = todo.pop(0)
            order.append(("run", name))
            log.append((round(t, 1), name))
            t += cost
        elif heap:
            t = max(t, heap[0][0])
    return order, t, log


def columns_of(slab, part):
    buf, first, tiles = SLABS[slab]
    start = first + sum(tiles[:part])
    return buf, slice(start * TILE, (start + tiles[part]) * TILE)


def make_comm(bufs, inputs, send_sem, recv_sem):
    dp, mp = lax.axis_index("dp"), lax.axis_index("mp")
    me = {"x": mp % 4, "y": mp // 4, "z": dp // 2}
    core = dp % 2
    partner = (me["z"] * 2 + 1 - core, mp)

    def at(axis, step):
        return (me[axis] + step) % 4

    def device(axis, step):
        pos = dict(me)
        pos[axis] = at(axis, step)
        return (pos["z"] * 2 + core, pos["y"] * 4 + pos["x"])

    slices = {"all": slice(0, 4), "low": slice(0, 2), "high": slice(2, 4)}

    def region(slab, part, spec, which_core):
        buf, cols = columns_of(slab, part)
        pos = {a: slices[s] if s in slices else at(a, s) for a, s in zip(ORDERS[part], spec)}
        return bufs[buf].at[pos["z"], which_core, pos["y"], pos["x"], :, cols]

    def copy(slab, part, e, received, source=None):
        stage, step, spec, _ = event_of(slab, part, e)
        other = core
        if stage == 4:
            target, other = partner, 1 - core
        else:
            target = device(ORDERS[part][stage - 1], step)
        if received and stage < 4:
            spec = tuple(s - step if i == stage - 1 else s for i, s in enumerate(spec))
        ref = region(slab, part, spec, other if received else core)
        k = (slab * 3 + part) * EVENTS + e
        return pltpu.make_async_remote_copy(
            src_ref=ref if source is None else source, dst_ref=ref, send_sem=send_sem.at[k], recv_sem=recv_sem.at[k],
            device_id=target, device_id_type=MESH,
        )

    def send(slab, part, e):
        if event_of(slab, part, e)[2] != (0, 0, 0):
            copy(slab, part, e, False).start()
            return
        buf, cols = columns_of(slab, part)
        qk, v, o, down, up = inputs
        if buf == 0:
            for c, adapters in ((0, down), (1, up)):

                @pl.when(core == c)
                def _(adapters=adapters):
                    copy(slab, part, e, False, adapters.at[me["z"], :, cols]).start()

        elif buf == 2:
            copy(slab, part, e, False, o.at[:, cols]).start()
        elif cols.start < 512:
            copy(slab, part, e, False, qk.at[:, cols]).start()
        else:
            copy(slab, part, e, False, v.at[:, cols.start - 512 : cols.stop - 512]).start()

    def recv(slab, part, e):
        copy(slab, part, e, True).wait_recv()

    def finish():
        for slab in range(len(SLABS)):
            for part in range(3):
                for e in range(EVENTS):
                    copy(slab, part, e, False).wait_send()

    def barrier():
        sem = pltpu.get_barrier_semaphore()
        for axis in "xyz":
            for step in (1, -1):
                pl.semaphore_signal(sem, inc=1, device_id=device(axis, step), device_id_type=MESH)
        pl.semaphore_signal(sem, inc=1, device_id=partner, device_id_type=MESH)
        return lambda: pl.semaphore_wait(sem, 7)

    return me, core, send, recv, finish, barrier


def own_copies(me, core, qk, v, o, down, up, bufs, sems):
    z, y, x = me["z"], me["y"], me["x"]
    a_buf, v_buf, o_buf = bufs
    adapter = a_buf.at[z, core, y, x]

    @pl.when(core == 0)
    def _():
        pltpu.make_async_copy(down.at[z], adapter, sems.at[0]).start()

    @pl.when(core == 1)
    def _():
        pltpu.make_async_copy(up.at[z], adapter, sems.at[0]).start()

    copies = [
        pltpu.make_async_copy(qk, v_buf.at[z, core, y, x, :, 0:512], sems.at[1]),
        pltpu.make_async_copy(v, v_buf.at[z, core, y, x, :, 512 : 512 + WIDTH], sems.at[2]),
        pltpu.make_async_copy(o, o_buf.at[z, core, y, x], sems.at[3]),
    ]
    for c in copies:
        c.start()

    def wait():
        pltpu.make_async_copy(down.at[z], adapter, sems.at[0]).wait()
        for c in copies:
            c.wait()

    return wait


def dot(a, b):
    return jnp.dot(a, b, preferred_element_type=F32)


def dot_t(a, b):
    return lax.dot_general(a, b, (((1,), (1,)), ((), ())), preferred_element_type=F32)


def kernel(
    order, lengths_in, adapters_in, stream, gain_in, qk, v, o, taps_in, down, up, out,
    a_buf, v_buf, o_buf, x_buf, normed, values, qk_buf, attended, sel_down, sel_up, low_buf, mixed, mask, same,
    weights0, weights1, lengths, adapters, gain, taps, send_sem, recv_sem, local_sem,
):
    bufs = (a_buf, v_buf, o_buf)
    me, core, send, recv, finish, barrier = make_comm(bufs, (qk, v, o, down, up), send_sem, recv_sem)
    wait_neighbours = barrier()
    wait_own = own_copies(me, core, qk, v, o, down, up, bufs, local_sem)
    stream_in = pltpu.make_async_copy(stream, x_buf, local_sem.at[4])
    stream_in.start()
    small = [
        pltpu.make_async_copy(s, d, local_sem.at[5 + i])
        for i, (s, d) in enumerate(((lengths_in, lengths), (adapters_in, adapters), (gain_in, gain), (taps_in, taps)))
    ]
    for c in small:
        c.start()
    wait_neighbours()

    def tile(buf, start, width):
        cols = pl.ds(pl.multiple_of(start, 128), width)
        return buf[:, :, :, :, :, cols].reshape(2048, width)

    def norm():
        stream_in.wait()
        for c in small:
            c.wait()

        def rows(i, _):
            r = pl.ds(pl.multiple_of(i * 32, 32), 32)
            x = x_buf[r, :].astype(F32)
            mean_sq = jnp.mean(x * x, axis=1, keepdims=True)
            normed[r, :] = (x * lax.rsqrt(mean_sq + NORM_EPS) * gain[...]).astype(BF16)
            return 0

        lax.fori_loop(0, TOK // 32, rows, 0)

    def masks():
        bounds, total = [], 0
        for k in range(8):
            total = total + lengths[0, k]
            bounds.append(total)

        def rows(i, _):
            r = pl.ds(pl.multiple_of(i * 64, 64), 64)

            def start_of(width):
                t = lax.broadcasted_iota(jnp.int32, (64, width), 0) + i * 64
                first = jnp.zeros((64, width), jnp.int32)
                for b in bounds:
                    first = jnp.where(t >= b, b, first)
                return t, first

            t, first = start_of(512)
            s = lax.broadcasted_iota(jnp.int32, (64, 512), 1)
            mask[r, :] = jnp.where((s <= t) & (s >= first), 0.5, 0.0).astype(F32)
            t, first = start_of(128)
            same[0, r, :] = jnp.where(t - 1 >= first, 1.0, 0.0).astype(F32)
            same[1, r, :] = jnp.where(t - 2 >= first, 1.0, 0.0).astype(F32)
            return 0

        lax.fori_loop(0, TOK // 64, rows, 0)

    def project_qk():
        def one(i, _):
            c = pl.ds(pl.multiple_of(i * 256, 256), 256)
            qk_buf[:, c] = dot(normed[...], tile(v_buf, i * 256, 256)).astype(BF16)
            return 0

        lax.fori_loop(0, 2, one, 0)

    def project_v(first, count):
        def one(i, _):
            c = pl.ds(pl.multiple_of(i * 256, 256), 256)
            values[:, c] = dot(normed[...], tile(v_buf, 512 + i * 256, 256))
            return 0

        lax.fori_loop(first, first + count, one, 0)

    def low_rank():
        for b in range(TOK // BLK):
            a = adapters[b]
            z, m = lax.rem(a, 4), lax.div(a, 4)
            y, x = lax.div(m, 4), lax.rem(m, 4)
            sel_down[b * 16 : (b + 1) * 16, :] = a_buf[z, 0, y, x]
            sel_up[b * 16 : (b + 1) * 16, :] = a_buf[z, 1, y, x]
        low = dot_t(normed[...], sel_down[...])
        block = lax.broadcasted_iota(jnp.int32, (TOK, 256), 0) // BLK
        owner = lax.broadcasted_iota(jnp.int32, (TOK, 256), 1) // 16
        low_buf[...] = (2.0 * jnp.where(block == owner, low, 0.0)).astype(BF16)

    def gate(first, count):
        def one(i, _):
            c = pl.ds(pl.multiple_of(i * 256, 256), 256)
            fix = dot(low_buf[...], sel_up[:, c])
            for half in range(2):
                c = pl.ds(pl.multiple_of(i * 256 + half * 128, 128), 128)
                val = values[:, c] + fix[:, half * 128 : (half + 1) * 128].astype(BF16).astype(F32)
                conv = taps[0:1, c] * val
                conv = conv + taps[1:2, c] * (pltpu.roll(val, 1, axis=0) * same[0])
                conv = conv + taps[2:3, c] * (pltpu.roll(val, 2, axis=0) * same[1])
                mixed[:, c] = (conv * (val / (1.0 + jnp.exp(-val)))).astype(BF16)
            return 0

        lax.fori_loop(first, first + count, one, 0)

    blocks = ((0, 256, 256), (256, 512, 512))

    def scores(first, count):
        def one(i, _):
            group = pl.multiple_of(i // 2 * 128, 128)
            lane_head = lax.broadcasted_iota(jnp.int32, (TOK, 128), 1) // 16
            quarter = qk_buf[:, pl.ds(group, 128)] * 0.25
            k = qk_buf[:, pl.ds(256 + group, 128)]
            for n in range(4):
                h = i * 4 + n
                q = jnp.where(lane_head == h % 8, quarter, 0.0).astype(BF16)
                for (r0, r1, k1), store in zip(blocks, (weights0, weights1)):
                    u1 = dot_t(q[r0:r1], k[:k1]) + 1.0
                    store[h] = ((u1 * u1 + 1.0) * mask[r0:r1, :k1]).astype(BF16)
            return 0

        lax.fori_loop(first, first + count, one, 0)

    def attend(first, count):
        def one(i, _):
            for n in range(4):
                h = i * 4 + n
                c = pl.ds(pl.multiple_of(h * 128, 128), 128)
                right = jnp.concatenate([mixed[:, c], jnp.ones((TOK, 128), BF16)], axis=1)
                for (r0, r1, k1), store in zip(blocks, (weights0, weights1)):
                    both = dot(store[h], right[:k1])
                    attended[r0:r1, c] = (both[:, :128] / both[:, 128:]).astype(BF16)
            return 0

        lax.fori_loop(first, first + count, one, 0)

    out_copies = []

    def project_out(first, count):
        def one(i, _):
            c = pl.ds(pl.multiple_of(i * 256, 256), 256)
            x_buf[:, c] = (x_buf[:, c].astype(F32) + dot(attended[...], tile(o_buf, i * 256, 256))).astype(BF16)
            return 0

        lax.fori_loop(first, first + count, one, 0)
        c = slice(first * 256, (first + count) * 256)
        done = pltpu.make_async_copy(x_buf.at[:, c], out.at[:, c], local_sem.at[9 + len(out_copies)])
        done.start()
        out_copies.append(done)

    run = {"norm": norm, "masks": masks, "qk": project_qk, "low": low_rank}
    own_here = False
    for op in order:
        if op[0] == "send" and event_of(*op[1:])[2] != (0, 0, 0) and not own_here:
            wait_own()
            own_here = True
        if op[0] == "send":
            send(*op[1:])
        elif op[0] == "recv":
            recv(*op[1:])
        elif op[1] in run:
            run[op[1]]()
        else:
            {"v": project_v, "g": gate, "s": scores, "h": attend, "o": project_out}[op[1][0]](*op[1][1:])
    finish()
    for c in out_copies:
        c.wait()


PIECES = [
    ("norm", (), 1.5),
    ("masks", (), 0.5),
    ("qk", (0,), 1.5),
    (("v", 0, 2), (0,), 1.5),
    (("v", 2, 2), (0,), 1.5),
    (("s", 0, 2), (), 1.6),
    (("s", 2, 2), (), 1.6),
    (("v", 4, 2), (1,), 1.5),
    (("v", 6, 2), (1,), 1.5),
    ("low", (2,), 0.8),
    (("g", 0, 4), (), 1.8),
    (("h", 0, 2), (), 1.5),
    (("g", 4, 4), (), 1.8),
    (("h", 2, 2), (), 1.5),
    (("o", 0, 2), (3,), 1.7),
    (("o", 2, 2), (3,), 1.7),
    (("o", 4, 2), (4,), 1.7),
    (("o", 6, 2), (4,), 1.7),
]


def local(
    stream, norm_weight, query_key_weight, value_weight, output_weight, convolution_weights,
    adapter_down_maps, adapter_up_maps, prompt_lengths, block_adapter_index,
):
    order = plan(PIECES)[0]
    n = len(SLABS) * 3 * EVENTS
    any_, hbm = pl.BlockSpec(memory_space=pl.ANY), pl.BlockSpec(memory_space=pltpu.HBM)
    return pl.pallas_call(
        lambda *refs: kernel(order, *refs),
        out_shape=jax.ShapeDtypeStruct((TOK, WIDTH), BF16),
        in_specs=[hbm] * 10,
        out_specs=any_,
        scratch_shapes=[pltpu.VMEM(s, BF16) for s in SHAPES]
        + [
            pltpu.VMEM((TOK, WIDTH), BF16),
            pltpu.VMEM((TOK, WIDTH), BF16),
            pltpu.VMEM((TOK, WIDTH), F32),
            pltpu.VMEM((TOK, 512), BF16),
            pltpu.VMEM((TOK, WIDTH), BF16),
            pltpu.VMEM((256, WIDTH), BF16),
            pltpu.VMEM((256, WIDTH), BF16),
            pltpu.VMEM((TOK, 256), BF16),
            pltpu.VMEM((TOK, WIDTH), BF16),
            pltpu.VMEM((TOK, TOK), F32),
            pltpu.VMEM((2, TOK, 128), F32),
            pltpu.VMEM((HEADS, 256, 256), BF16),
            pltpu.VMEM((HEADS, 256, 512), BF16),
            pltpu.SMEM((1, 8), jnp.int32),
            pltpu.SMEM((TOK // BLK,), jnp.int32),
            pltpu.VMEM((1, WIDTH), F32),
            pltpu.VMEM((3, WIDTH), F32),
            pltpu.SemaphoreType.DMA((n,)),
            pltpu.SemaphoreType.DMA((n,)),
            pltpu.SemaphoreType.DMA((16,)),
        ],
        compiler_params=pltpu.CompilerParams(
            collective_id=0, has_side_effects=True, vmem_limit_bytes=51 << 20
        ),
        name="layer",
    )(*[pltpu.with_memory_space_constraint(a, pltpu.HBM) for a in (
        prompt_lengths, block_adapter_index, stream, norm_weight.reshape(1, WIDTH), query_key_weight,
        value_weight, output_weight, convolution_weights, adapter_down_maps, adapter_up_maps,
    )])


def solution(mesh):
    rows, whole = P(("dp", "mp"), None), P()
    return jax.shard_map(
        local,
        mesh=mesh,
        in_specs=(
            rows, whole, rows, rows, rows, whole, P("mp", None, None), P("mp", None, None), rows, P(("dp", "mp")),
        ),
        out_specs=rows,
        check_vma=False,
    )
```

time: 91.5 us -> 78.2 us (0.85)
  Pallas kernels: 88.1 us -> 76.7 us
  local copies, waits for them, and re-layouts: 3.16 us -> 1.32 us
    pallas_call x1, Pallas kernels: 88.1 us -> 76.7 us  [local(): pl.pallas_call(lambda *refs: kernel(order, *refs), out_shape=jax.ShapeDty...]
    unnamed x1, local copies, waits for them, and re-layouts: 3.16 us -> 1.32 us
where the time goes in v3:
time: 78.2 us; the launch traced here: 78.1 us
  Pallas kernels  76.7 us (98%)
  local copies, waits for them, and re-layouts  1.32 us (2%)
    pallas_call x1, Pallas kernels, local(): pl.pallas_call(lambda *refs: kernel(order, *refs), out_shape=jax.ShapeDty...  76.7 us

profile of v3, /device:TPU:1, one launch (start us, length us, event | category | flops | bytes accessed | tf_op | source)
XLA Modules:
  0.0 78.1 jit_solution(14647740542334452584)
XLA Ops:
  0.0 76.7 %layer.1 = bf16[512,2048]{1,0:T(8,128)(2,1)S(1)} custom-call(s32[1,8]{1,0:T(1,128)} %refs_0_.1, s32[16]{0:T(128)} %refs_1_.1, bf16[512,2048]{1,0:T(8,128)(2,1)} %refs_2_.1, f32[1,2048]{1,0:T(1,128)} %bitcast.1, bf16[16,512]{1,0:T(8,128)(2,1)} %refs_4_.1, bf16[16,2048]{1,0:T(8,128)(2,1)} %refs_5_.1, bf16[16,2048]{1,0:T(8,128)(2,1)} %refs_6_.1, ...), custom_call_target="tpu_custom_call" | custom-call | tf_op jit(solution)/shard_map/layer/pallas_call | solution.py:444
  76.7 1.3 %copy.12 = bf16[512,2048]{1,0:T(8,128)(2,1)} copy(bf16[512,2048]{1,0:T(8,128)(2,1)S(1)} %layer.1) | data formatting | bytes 4194304

commit v4 on v3

--- a/solution.py
+++ b/solution.py
@@ -52,17 +52,23 @@
         ev.append((2, 1, ("low", -1, 0), (3,)))
         ev.append((2, -1, ("high", 1, 0), (4,)))
         stage2 = (0, 1, 2, 3, 4, 5, 6)
-        ev.append((3, 1, ("low", "all", 0), stage2))
-        ev.append((3, -1, ("high", "all", 0), stage2))
-        ev.append((3, 1, ("high", "all", 0), stage2))
-        ev.append((3, -1, ("low", "all", 0), stage2))
+        if fine is None:
+            ev.append((3, 1, ("all", "all", 0), stage2))
+            ev.append((3, -1, ("all", "all", 0), stage2))
+            near, far = ((7,), (8,)), (9, 10)
+        else:
+            ev.append((3, 1, ("low", "all", 0), stage2))
+            ev.append((3, -1, ("high", "all", 0), stage2))
+            ev.append((3, 1, ("high", "all", 0), stage2))
+            ev.append((3, -1, ("low", "all", 0), stage2))
+            near, far = ((7, 9), (8, 10)), (11, 12)
         ev.append((3, 1, ("low", "all", -1), (7,)))
         ev.append((3, -1, ("high", "all", 1), (8,)))
         ev.append((4, 0, ("all", "all", 0), stage2))
-        ev.append((4, 0, ("all", "all", -1), (7, 9)))
-        ev.append((4, 0, ("all", "all", 1), (8, 10)))
-        ev.append((4, 0, ("low", "all", 2), (11,)))
-        ev.append((4, 0, ("high", "all", 2), (12,)))
+        ev.append((4, 0, ("all", "all", -1), near[0]))
+        ev.append((4, 0, ("all", "all", 1), near[1]))
+        ev.append((4, 0, ("low", "all", 2), far[:1]))
+        ev.append((4, 0, ("high", "all", 2), far[1:]))
     return ev
 
 
@@ -88,7 +94,7 @@
     return units * SLABS[slab][2][part] * 16 * TILE * 2
 
 
-def plan(pieces, rate=46e3, partner_rate=480e3, latency=1.8, depth=2.0, early=1):
+def plan(pieces, rate=46e3, partner_rate=480e3, latency=1.8, depth=3.0, early=1):
     free, heap, order, log = {}, [], [], []
     got = [[set() for _ in range(3)] for _ in SLABS]
     waiting = [(s, p, e) for s in range(len(SLABS)) for p in range(3) for e in range(EVENTS)]
@@ -343,7 +349,7 @@
                 conv = taps[0:1, c] * val
                 conv = conv + taps[1:2, c] * (pltpu.roll(val, 1, axis=0) * same[0])
                 conv = conv + taps[2:3, c] * (pltpu.roll(val, 2, axis=0) * same[1])
-                mixed[:, c] = (conv * (val / (1.0 + jnp.exp(-val)))).astype(BF16)
+                mixed[:, c] = (conv * (0.5 * val * (1.0 + jnp.tanh(0.5 * val)))).astype(BF16)
             return 0
 
         lax.fori_loop(first, first + count, one, 0)
@@ -467,7 +473,7 @@
             pltpu.VMEM((3, WIDTH), F32),
             pltpu.SemaphoreType.DMA((n,)),
             pltpu.SemaphoreType.DMA((n,)),
-            pltpu.SemaphoreType.DMA((16,)),
+            pltpu.SemaphoreType.DMA((24,)),
         ],
         compiler_params=pltpu.CompilerParams(
             collective_id=0, has_side_effects=True, vmem_limit_bytes=51 << 20

time: 78.2 us -> 77.8 us (level)
  no operation moved by 1% of the time
where the time goes in v4:
time: 77.8 us; the launch traced here: 77.7 us
  Pallas kernels  76.4 us (98%)
  local copies, waits for them, and re-layouts  1.32 us (2%)
    pallas_call x1, Pallas kernels, local(): pl.pallas_call(lambda *refs: kernel(order, *refs), out_shape=jax.ShapeDty...  76.4 us

profile of v4, /device:TPU:1, one launch (start us, length us, event | category | flops | bytes accessed | tf_op | source)
XLA Modules:
  0.0 77.7 jit_solution(7564354668742794500)
XLA Ops:
  0.0 76.4 %layer.1 = bf16[512,2048]{1,0:T(8,128)(2,1)S(1)} custom-call(s32[1,8]{1,0:T(1,128)} %refs_0_.1, s32[16]{0:T(128)} %refs_1_.1, bf16[512,2048]{1,0:T(8,128)(2,1)} %refs_2_.1, f32[1,2048]{1,0:T(1,128)} %bitcast.1, bf16[16,512]{1,0:T(8,128)(2,1)} %refs_4_.1, bf16[16,2048]{1,0:T(8,128)(2,1)} %refs_5_.1, bf16[16,2048]{1,0:T(8,128)(2,1)} %refs_6_.1, ...), custom_call_target="tpu_custom_call" | custom-call | tf_op jit(solution)/shard_map/layer/pallas_call | solution.py:450
  76.4 1.3 %copy.12 = bf16[512,2048]{1,0:T(8,128)(2,1)} copy(bf16[512,2048]{1,0:T(8,128)(2,1)S(1)} %layer.1) | data formatting | bytes 4194304
